TPU v7x, 32 devices: a whole 2x2x4 slice. The times are simulated.
32 devices in a mesh: dom: 16 (over z, y, x), wav: 2 (over core).
Axes of the slice: x: 2, y: 2, z: 4, core: 2. Of those that a mesh axis runs over, the one named last changes fastest.
Arguments:
- node_features: bfloat16 [16384, 128], P('dom'), may hold values from -6 to 6
- positions: float32 [3, 16384], P(None, 'dom'), may hold values from 0 to 1, as said below
- neighbours: int32 [128, 8], P('dom'), may hold values from 0 to 15, as said below
- wavevectors: int32 [3, 8192], P(None, 'wav'), may hold values from -8 to 8
- message_weight: bfloat16 [1, 128, 128], replicated, may hold values from -0.5 to 0.5
- spectral_mix: float32 [1, 128, 128], replicated, may hold values from -0.5 to 0.5
- spectral_filter: float32 [1, 8192, 128], P(None, 'wav'), may hold values from 0.2 to 2
Outputs:
- features_out: bfloat16 [16384, 128], P('dom')
Inputs may be any that keep to these rules, and one draw needn't show every extreme that they name: `positions`: atom a lies in the unit box with its first coordinate in [d / (number of domains), (d + 1) / (number of domains)) for d = a // 1024; the box is periodic. `neighbours`: each row names 8 different blocks, within 4 places of the row's own block (b mod 8) + 4 in the extended list.
All inputs are finite; a program needn't handle non-finite values.
Results may differ from a plain program's by a relative error of at most 0.0045.
Values may be sent and summed in bfloat16 or wider, within the bound.
No kernel may reach another device: no remote copies, remote signals or barrier semaphores. Data moves between devices by JAX's collectives and lax.ppermute only.
A program may use at most 64 MiB of HBM per device.

v0:
```python
import math

import jax
import jax.numpy as jnp
from jax import lax
from jax.experimental import pallas as pl
from jax.experimental.pallas import tpu as pltpu
from jax.sharding import PartitionSpec as P


KV = 8192
BLOCK = 128
NBR = 8
HALO_BLK = 4
TOP = 8
SPAN = 2 * TOP + 1

TWO_PI = 2.0 * math.pi
KERNEL_DECAY = 12.0
PAIR_SCALE = 1.0 / 16.0

TILE = 8
CHAINS = 2
Q_TILES = 2 * SPAN + 3
Q_ROWS = Q_TILES * TILE
FIRST_TILE = 2 + 2 * TOP
ZERO_TILES = Q_TILES - FIRST_TILE
ALL_TILES = ZERO_TILES + TOP * Q_TILES
assert TOP == TILE

F32 = jnp.float32
BF16 = jnp.bfloat16
VMEM = pltpu.VMEM


def in_vmem(array):
    return pltpu.with_memory_space_constraint(array, VMEM)


def call(body, out, *args, smem=(), scratch=(), limit=16):
    spec = pl.BlockSpec(memory_space=VMEM)
    specs = [spec] * len(args) + [pl.BlockSpec(memory_space=pltpu.SMEM)] * len(smem)
    single = not isinstance(out, (list, tuple))
    return pl.pallas_call(
        body,
        in_specs=specs,
        out_specs=spec if single else [spec] * len(out),
        out_shape=out,
        scratch_shapes=list(scratch),
        compiler_params=pltpu.CompilerParams(vmem_limit_bytes=limit << 20),
    )(*[in_vmem(a) for a in args], *smem)


DIVIDE = -(-(1 << 16) // Q_TILES)
assert all((v * DIVIDE) >> 16 == v // Q_TILES for v in range(ALL_TILES))


class Layout:
    def __init__(self, atoms):
        self.atoms = atoms
        self.doms, self.wavs = lax.axis_size("dom"), lax.axis_size("wav")
        self.bits = self.doms.bit_length() - 1
        assert self.doms == 1 << self.bits and self.bits > 3
        assert self.wavs & (self.wavs - 1) == 0
        self.tiles = -(-ALL_TILES // (self.doms * self.wavs * CHAINS))
        self.slice_rows = 2 * TILE * self.tiles
        self.rows = self.slice_rows * self.doms

    def order(self, wav, chain):
        turn = (0, 1, 2, 0)[(CHAINS * wav + chain) % 4]
        first = [0, 1, 2]
        return first[turn:] + first[:turn] + list(range(3, self.bits))

    def code(self, wav, chain):
        dom = lax.axis_index("dom")
        codes = []
        for w in (0, 1):
            code = 0
            for step, bit in enumerate(self.order(w, chain)):
                code = code | (((dom >> bit) & 1) << (self.bits - 1 - step))
            codes.append(code)
        return jnp.where((wav & 1) == 0, codes[0], codes[1])

    def first_tile(self, wav, chain, position):
        number = CHAINS * wav + chain
        return (number * self.doms + (position ^ self.code(wav, chain))) * self.tiles


def tile_place(tile):
    tile = jnp.minimum(tile, ALL_TILES - 1)
    later = tile - ZERO_TILES
    first = later < 0
    plane = (jnp.maximum(later, 0) * DIVIDE) >> 16
    n2 = jnp.where(first, 0, 1 + plane)
    return n2, jnp.where(first, FIRST_TILE + tile, later - plane * Q_TILES)


def times(a, b):
    return a[0] * b[0] - a[1] * b[1], a[0] * b[1] + a[1] * b[0]


def fill_tables(pos_ref, xyc_ref, xys_ref, zc_ref, zs_ref):
    angle = TWO_PI * pos_ref[...]
    power = [(jnp.ones_like(angle), jnp.zeros_like(angle)), (jnp.cos(angle), jnp.sin(angle))]
    for n in range(2, TOP + 1):
        power.append(times(power[n // 2], power[n - n // 2]))
    wide = (TILE, angle.shape[1])

    def row(n, axis):
        c, s = power[abs(n)]
        c, s = c[axis : axis + 1, :], s[axis : axis + 1, :]
        return c, (s if n >= 0 else -s)

    def spread(n, axis):
        return tuple(jnp.broadcast_to(v, wide) for v in row(n, axis))

    def stack(numbers, axis):
        rows = [row(n, axis) for n in numbers]
        return tuple(jnp.concatenate([r[i] for r in rows], axis=0) for i in (0, 1))

    for n in range(TOP + 1):
        at = slice(n * TILE, (n + 1) * TILE)
        zc_ref[at, :], zs_ref[at, :] = spread(n, 2)

    def put(tile, a, b):
        at = slice(tile * TILE, (tile + 1) * TILE)
        xyc_ref[at, :], xys_ref[at, :] = times(a, b)

    below, above = stack(range(-TOP, 0), 1), stack(range(TOP), 1)
    edge = spread(TOP, 1)
    for n in range(-TOP, TOP + 1):
        here = spread(n, 0)
        put(1 + 2 * (n + TOP), here, below)
        put(2 + 2 * (n + TOP), here, above)
    put(0, stack(range(-TOP, 0), 0), edge)
    put(Q_TILES - 2, stack(range(TOP), 0), edge)
    put(Q_TILES - 1, spread(TOP, 0), edge)


def fill_phases(lay, chain, low, count, tables, h_ref, p_ref, p_at, put):
    xyc_ref, xys_ref, zc_ref, zs_ref = tables
    wav = lax.axis_index("wav")
    group = max(1, count // 2)
    rows = group * lay.slice_rows
    feats = h_ref[...]

    def chunk(step, carry):
        start = pl.multiple_of(step * rows, rows)
        for part in range(group):
            base = lay.first_tile(wav, chain, low + step * group + part)
            for i in range(lay.tiles):
                n2, qt = tile_place(base + i)
                q_at = pl.ds(pl.multiple_of(qt * TILE, TILE), TILE)
                z_at = pl.ds(pl.multiple_of(n2 * TILE, TILE), TILE)
                c, s = times((xyc_ref[q_at, :], xys_ref[q_at, :]), (zc_ref[z_at, :], zs_ref[z_at, :]))
                at = p_at + start + (part * lay.tiles + i) * 2 * TILE
                at = pl.ds(pl.multiple_of(at, 2 * TILE), 2 * TILE)
                p_ref[at, :] = jnp.concatenate([c, s], axis=0).astype(BF16)
        here = pl.ds(pl.multiple_of(p_at + start, rows), rows)
        put(pl.ds(start, rows), jnp.dot(p_ref[here, :], feats, preferred_element_type=F32))
        return carry

    lax.fori_loop(0, count // group, chunk, 0)


def phase_tables(positions):
    atoms = positions.shape[1]
    table = [(Q_ROWS, atoms)] * 2 + [((TOP + 1) * TILE, atoms)] * 2
    return call(fill_tables, [VMEM(shape, F32) for shape in table], positions)


def spectrum_upper(lay, chain, scale, tables, features):
    half = lay.doms // 2

    def body(xyc, xys, zc, zs, h_ref, p_ref, s_ref):
        def put(at, value):
            s_ref[at, :] = (value * scale).astype(BF16)

        fill_phases(lay, chain, half, half, (xyc, xys, zc, zs), h_ref, p_ref, 0, put)

    out = [VMEM((lay.rows // 2, lay.atoms), BF16), VMEM((lay.rows // 2, features.shape[1]), BF16)]
    return call(body, out, *tables, features)


def spectrum_lower(lay, scale, tables, features):
    def body(xyc, xys, zc, zs, h_ref, p_ref, *s_refs):
        for chain, s_ref in enumerate(s_refs):

            def put(at, value):
                s_ref[at, :] = value * scale

            fill_phases(
                lay, chain, 0, lay.doms // 2, (xyc, xys, zc, zs), h_ref, p_ref,
                chain * (lay.rows // 2), put,
            )

    out = [VMEM((CHAINS * lay.rows // 2, lay.atoms), BF16)]
    out += [VMEM((lay.rows // 2, features.shape[1]), F32)] * CHAINS
    phases, *sums = call(body, out, *tables, features)
    return phases, sums


def lattice_weights(lay, wavevectors, weights):
    waves, channels = weights.shape
    tiles = 2 * lay.tiles * lay.wavs * CHAINS
    chunk = min(waves, 1024)

    def body(wave_ref, filter_ref, *refs):
        *out_refs, hot_ref = refs
        wav = lax.axis_index("wav")
        bases = []
        for v in range(lay.wavs):
            for chain in range(CHAINS):
                for p in range(2):
                    first = lay.first_tile(wav ^ v, chain, p)
                    for i in range(lay.tiles):
                        n2, qt = tile_place(first + i)
                        base = n2 * Q_ROWS + qt * TILE
                        bases.append(jnp.where(first + i < ALL_TILES, base, -Q_ROWS))
        total = None
        for start in range(0, waves, chunk):
            at = slice(start, start + chunk)
            n0, n1, n2 = (wave_ref[a : a + 1, at] for a in range(3))
            negative = jnp.logical_or(n0 < 0, jnp.logical_and(n0 == 0, n1 < 0))
            flip = jnp.logical_or(n2 < 0, jnp.logical_and(n2 == 0, negative))
            n0, n1, n2 = (jnp.where(flip, -n, n) for n in (n0, n1, n2))
            inner = TILE + (n0 + TOP) * 2 * TILE + n1 + TOP
            outer = jnp.where(n0 < 0, n0 + TOP, (Q_TILES - 2) * TILE + n0)
            key = n2 * Q_ROWS + jnp.where(n1 == TOP, outer, inner)
            wide = jnp.broadcast_to(key, (TILE, chunk))
            shifted = wide - lax.broadcasted_iota(jnp.int32, wide.shape, 0)
            for t in range(0, tiles, 2):
                both = [jnp.where(shifted == bases[u], 1.0, 0.0) for u in (t, t + 1)]
                hot_ref[t * TILE : (t + 2) * TILE, :] = jnp.concatenate(both, axis=0).astype(BF16)
            w = filter_ref[at, :]
            high = w.astype(BF16)
            low = (w - high.astype(F32)).astype(BF16)
            part = jnp.dot(
                hot_ref[...], jnp.concatenate([high, low], axis=1), preferred_element_type=F32
            )
            total = part if total is None else total + part
        total = total[:, :channels] + total[:, channels:]
        rows = tiles * TILE // lay.wavs
        for v, ref in enumerate(out_refs):
            ref[...] = total[v * rows : (v + 1) * rows]

    out = [VMEM((tiles * TILE // lay.wavs, channels), F32)] * lay.wavs
    return call(
        body, out, wavevectors, weights,
        scratch=[VMEM((tiles * TILE, chunk), BF16)],
    )


def add_split(mine, other):
    rows, channels = mine.shape

    def body(a_ref, b_ref, keep_ref, send_ref):
        total = a_ref[...] + b_ref[...].astype(F32)
        keep_ref[...] = total[: rows // 2]
        send_ref[...] = total[rows // 2 :].astype(BF16)

    out = [VMEM((rows // 2, channels), F32), VMEM((rows // 2, channels), BF16)]
    return call(body, out, mine, other)


def add_all(mine, others):
    rows, channels = mine[0].shape

    def body(*refs):
        keep_ref, send_ref = refs[-2:]
        for i in range(CHAINS):
            at = slice(i * rows, (i + 1) * rows)
            total = refs[i][...] + refs[CHAINS + i][...].astype(F32)
            keep_ref[at, :] = total
            send_ref[at, :] = total.astype(BF16)

    out = [VMEM((CHAINS * rows, channels), t) for t in (F32, BF16)]
    return call(body, out, *mine, *others)


def add_plain(mine, other):
    def body(a_ref, b_ref, out_ref):
        out_ref[...] = a_ref[...] + b_ref[...].astype(F32)

    return call(body, VMEM(mine.shape, F32), mine, other)


def dot_exact(a, b):
    return jnp.dot(a, b, precision=lax.Precision.HIGHEST, preferred_element_type=F32)


def filtered(mine, other, mixing, weights):
    rows, channels = mine.shape
    part = rows // CHAINS
    groups = rows // (2 * TILE)

    def body(mine_ref, other_ref, mix_ref, *refs):
        weight_refs, out_refs = refs[:-CHAINS], refs[-CHAINS:]
        there = other_ref[...].astype(F32)
        cuts = [there[i * part // 2 : (i + 1) * part // 2] for i in range(2 * CHAINS)]
        there = jnp.concatenate([cuts[i ^ 1] for i in range(2 * CHAINS)], axis=0)
        mixed = dot_exact(mine_ref[...] + there, mix_ref[...])
        factor = weight_refs[0][...]
        for ref in weight_refs[1:]:
            factor = factor + ref[...]
        mixed = mixed.reshape(groups, 2, TILE, channels) * factor.reshape(groups, 1, TILE, channels)
        mixed = mixed.reshape(rows, channels).astype(BF16)
        for i, ref in enumerate(out_refs):
            ref[...] = mixed[i * part : (i + 1) * part]

    out = [VMEM((part, channels), BF16)] * CHAINS
    return call(body, out, mine, other, mixing, *weights)


def join(low, high):
    def body(a_ref, b_ref, out_ref):
        rows = a_ref.shape[0]
        out_ref[:rows, :] = a_ref[...]
        out_ref[rows:, :] = b_ref[...]

    out = VMEM((low.shape[0] + high.shape[0], low.shape[1]), low.dtype)
    return call(body, out, low, high)


def pack_half(positions, features, share):
    rows, channels = share * BLOCK, features.shape[1]
    extra = -(-9 * share // (2 * TILE)) * 2 * TILE

    def body(pos_ref, h_ref, out_ref):
        start = pl.multiple_of(lax.axis_index("wav") * rows, rows)
        out_ref[:rows, :] = h_ref[pl.ds(start, rows), :]
        fill_coordinates(pos_ref[:, pl.ds(start, rows)], out_ref, rows)

    return call(body, VMEM((rows + extra, channels), BF16), positions, features)


def short_range(neighbours, positions, features, halos, weight, share):
    channels = features.shape[1]
    own = features.shape[0] // BLOCK
    near = [HALO_BLK] * len(halos)
    blocks = own + sum(near)
    both = len(halos) == 2

    def body(pos_ref, h_ref, weight_ref, *refs):
        halo_refs, (lists, out_ref, val_ref, at_ref) = refs[: len(halos)], refs[len(halos) :]
        w = weight_ref[...]

        def project(rows):
            return jnp.dot(rows, w, preferred_element_type=F32).astype(BF16)

        val_ref[: own * BLOCK, :] = project(h_ref[...])
        pos = pos_ref[...]
        for b in range(own):
            at_ref[b, 0:3, :] = pos[:, b * BLOCK : (b + 1) * BLOCK]
        at = own
        for ref, count in zip(halo_refs, near):
            rows = count * BLOCK
            val_ref[at * BLOCK : (at + count) * BLOCK, :] = project(ref[:rows, :])
            pieces = ref[rows:, :].astype(F32)
            n = 3 * count
            there = pieces[:n] + pieces[n : 2 * n] + pieces[2 * n : 3 * n]
            for b in range(count):
                for axis in range(3):
                    k = axis * count + b
                    at_ref[at + b, axis : axis + 1, :] = there[k : k + 1]
            at += count
        first = lax.axis_index("wav") * share

        def block(b, carry):
            columns = jnp.transpose(at_ref[first + b])
            total = jnp.zeros((BLOCK, channels), F32)
            for m in range(NBR):
                ext = lists[first + b, m]
                inside = jnp.logical_and(ext >= HALO_BLK, ext < HALO_BLK + own)
                if both:
                    outside = own + jnp.where(ext < HALO_BLK, ext, ext - own)
                else:
                    outside = own + jnp.where(ext < HALO_BLK, ext, ext - HALO_BLK - own)
                sender = jnp.where(inside, ext - HALO_BLK, outside)
                sent = at_ref[sender]
                distance = None
                for axis in range(3):
                    delta = columns[:, axis : axis + 1] - sent[axis : axis + 1, :]
                    delta = delta - jnp.floor(delta + 0.5)
                    square = delta * delta
                    distance = square if distance is None else distance + square
                kernel = jnp.exp(-KERNEL_DECAY * distance).astype(BF16)
                rows = pl.ds(pl.multiple_of(sender * BLOCK, BLOCK), BLOCK)
                total = total + jnp.dot(kernel, val_ref[rows, :], preferred_element_type=F32)
            out_ref[pl.ds(pl.multiple_of(b * BLOCK, BLOCK), BLOCK), :] = total * PAIR_SCALE
            return carry

        lax.fori_loop(0, share, block, 0)

    return call(
        body, VMEM((share * BLOCK, channels), F32), positions, features, weight,
        *halos, smem=[neighbours],
        scratch=[VMEM((blocks * BLOCK, channels), BF16), VMEM((blocks, TILE, BLOCK), F32)],
    )


def transposed_dot(phases, filt):
    dims = (((0,), (0,)), ((), ()))
    return lax.dot_general(phases, filt, dims, preferred_element_type=F32)


def back_lower(phases, filts):
    def body(p_ref, *refs):
        *f_refs, out_ref = refs
        filt = jnp.concatenate([ref[...] for ref in f_refs], axis=0)
        out_ref[...] = transposed_dot(p_ref[...], filt)

    out = VMEM((phases.shape[1], filts[0].shape[1]), F32)
    return call(body, out, phases, *filts)


def back_more(part, phases, filt):
    def body(part_ref, p_ref, f_ref, out_ref):
        out_ref[...] = part_ref[...] + transposed_dot(p_ref[...], f_ref[...])

    return call(body, VMEM(part.shape, F32), part, phases, filt)


def back_last(part, phases, filt, short, scale):
    rows = short.shape[0]

    def body(part_ref, p_ref, f_ref, short_ref, out_ref, send_ref):
        out_ref[...] = (part_ref[...] + transposed_dot(p_ref[...], f_ref[...])) * scale
        here = pl.ds(pl.multiple_of(lax.axis_index("wav") * rows, rows), rows)
        out_ref[here, :] += short_ref[...]
        send_ref[...] = out_ref[...].astype(BF16)

    out = [VMEM(part.shape, t) for t in (F32, BF16)]
    return call(body, out, part, phases, filt, short)


def finish(features, total, other):
    def body(h_ref, a_ref, b_ref, out_ref):
        total = a_ref[...] + b_ref[...].astype(F32)
        out_ref[...] = (h_ref[...].astype(F32) + total * jax.nn.sigmoid(total)).astype(BF16)

    out = jax.ShapeDtypeStruct(features.shape, BF16)
    return call(body, out, features, total, other)


def local(
    node_features, positions, neighbours, wavevectors, message_weight, spectral_mix, spectral_filter
):
    features = node_features
    atoms = features.shape[0]
    lay = Layout(atoms)
    doms, wavs, bits = lay.doms, lay.wavs, lay.bits
    blocks = atoms // BLOCK
    share = blocks // wavs
    inv_atoms = 1.0 / math.sqrt(atoms * doms)
    inv_waves = 1.0 / math.sqrt(KV)

    def swap(x, chain, step):
        pairs = []
        for d in range(doms):
            for w in range(wavs):
                pairs.append((d * wavs + w, (d ^ (1 << lay.order(w, chain)[step])) * wavs + w))
        return lax.ppermute(x, ("dom", "wav"), pairs)

    def swap_wav(x, mask):
        return lax.ppermute(x, "wav", [(w, w ^ mask) for w in range(wavs)])

    each = range(CHAINS)
    tables = phase_tables(positions)
    phases_up, arrived = [], []
    for c in each:
        phases, leaving = spectrum_upper(lay, c, inv_atoms, tables, features)
        phases_up.append(phases)
        arrived.append(swap(leaving, c, 0))
    phases_low, kept = spectrum_lower(lay, inv_atoms, tables, features)

    if wavs == 2 and share == HALO_BLK:
        packed = pack_half(positions, features, share)
        count = doms * wavs
        chain = [(g, (g + 1 if g % 2 else g - 1) % count) for g in range(count)]
        halos = [lax.ppermute(packed, ("dom", "wav"), chain)]
    else:
        halos = side_halos(positions, features)
    short = short_range(neighbours, positions, features, halos, message_weight[0], share)

    sums = list(lattice_weights(lay, wavevectors, spectral_filter[0]))
    mask = wavs // 2
    while mask:
        others = [swap_wav(s, mask) for s in sums[mask:]]
        if mask == 1:
            sums = [sums[0], *others]
        else:
            sums = [add_plain(a, b) for a, b in zip(sums[:mask], others)]
        mask //= 2

    for step in range(1, bits - 1):
        for c in each:
            kept[c], leaving = add_split(kept[c], arrived[c])
            arrived[c] = swap(leaving, c, step)
    total, leaving = add_all(kept, arrived)
    filts = list(filtered(total, swap(leaving, 0, bits - 1), spectral_mix[0], sums))
    for step in reversed(range(1, bits - 1)):
        for c in each:
            filts[c] = join(filts[c], swap(filts[c], c, step))
    filts_up = [swap(filts[c], c, 0) for c in each]
    part = back_lower(phases_low, filts)
    for c in range(CHAINS - 1):
        part = back_more(part, phases_up[c], filts_up[c])
    total, leaving = back_last(part, phases_up[-1], filts_up[-1], short, inv_waves)
    mask = wavs // 2
    while mask > 1:
        total = add_plain(total, swap_wav(total, mask))
        leaving = total
        mask //= 2
    return finish(features, total, swap_wav(leaving, 1))


def side_halos(positions, features):
    doms, atoms = lax.axis_size("dom"), features.shape[0]
    rim = HALO_BLK * BLOCK
    up = [(i, (i + 1) % doms) for i in range(doms)]
    down = [(j, i) for i, j in up]
    halos = []
    for at, pairs in ((atoms - rim, up), (0, down)):
        packed = pack_side(positions[:, at : at + rim], features[at : at + rim])
        halos.append(lax.ppermute(packed, "dom", pairs))
    return halos


def pack_side(positions, features):
    rows, channels = features.shape
    extra = -(-9 * HALO_BLK // (2 * TILE)) * 2 * TILE

    def body(pos_ref, h_ref, out_ref):
        out_ref[:rows, :] = h_ref[...]
        fill_coordinates(pos_ref[...], out_ref, rows)

    return call(body, VMEM((rows + extra, channels), BF16), positions, features)


def fill_coordinates(pos, out_ref, rows):
    high = pos.astype(BF16).astype(F32)
    mid = (pos - high).astype(BF16).astype(F32)
    parts = []
    for part in (high, mid, pos - high - mid):
        for axis in range(3):
            for b in range(rows // BLOCK):
                parts.append(part[axis : axis + 1, b * BLOCK : (b + 1) * BLOCK])
    parts += [jnp.zeros_like(parts[0])] * (out_ref.shape[0] - rows - len(parts))
    out_ref[rows:, :] = jnp.concatenate(parts, axis=0).astype(BF16)


def solution(mesh):
    placed = (
        P("dom", None),
        P(None, "dom"),
        P("dom", None),
        P(None, "wav"),
        P(),
        P(),
        P(None, "wav", None),
    )

    return jax.shard_map(local, mesh=mesh, in_specs=placed, out_specs=P("dom", None), check_vma=False)
```

profile of v0, /device:TPU:0, one launch (start us, length us, event | category | flops | bytes accessed | tf_op | source)
XLA Modules:
  0.0 54.6 jit_solution(8668789839236119676)
XLA Ops:
  0.0 0.0 copy-start.3
  0.0 0.7 %copy-done.3 = f32[3,1024]{1,0:T(4,128)S(1)} copy-done((f32[3,1024]{1,0:T(4,128)S(1)}, f32[3,1024]{1,0:T(4,128)}, u32[]{:S(2)}) %copy-start.3) | copy-done | bytes 12312
  0.7 0.5 shard_map.73
  1.3 0.0 copy-start
  1.3 0.9 %copy-done = bf16[1024,128]{1,0:T(8,128)(2,1)S(1)} copy-done((bf16[1024,128]{1,0:T(8,128)(2,1)S(1)}, bf16[1024,128]{1,0:T(8,128)(2,1)}, u32[]{:S(2)}) %copy-start) | copy-done | bytes 262168
  2.2 1.0 %shard_map.78 = (bf16[640,1024]{1,0:T(8,128)(2,1)S(1)}, bf16[640,128]{1,0:T(8,128)(2,1)S(1)}) custom-call(f32[296,1024]{1,0:T(8,128)S(1)} %get-tuple-element.32.xyc, f32[296,1024]{1,0:T(8,128)S(1)} %get-tuple-element.33.xys, f32[72,1024]{1,0:T(8,128)S(1)} %get-tuple-element.34.zc, f32[72,1024]{1,0:T(8,128)S(1)} %get-tuple-element.35.zs, ...), custom_call_target="tpu_custom_call" | custom-call | tf_op jit(solution)/shard_map/pallas_call | solution.py:44
  3.3 3.1 %collective-permute-start.2 = (bf16[640,128]{1,0:T(8,128)(2,1)S(1)}, bf16[640,128]{1,0:T(8,128)(2,1)S(1)}, u32[]{:S(2)}, u32[]{:S(2)}) collective-permute-start(bf16[640,128]{1,0:T(8,128)(2,1)S(1)} %get-tuple-element.43), channel_id=1, source_target_pairs={{0,4},{1,3},{2,6},{3,1},{4,0},{5,7},{6,2},{7,5},{8,12},{9,11},{10,... | collective-permute-start | bytes 491528 | tf_op jit(solution)/shard_map/ppermute | solution.py:463
  6.3 1.0 %shard_map.75 = (bf16[640,1024]{1,0:T(8,128)(2,1)S(1)}, bf16[640,128]{1,0:T(8,128)(2,1)S(1)}) custom-call(f32[296,1024]{1,0:T(8,128)S(1)} %get-tuple-element.32.xyc, f32[296,1024]{1,0:T(8,128)S(1)} %get-tuple-element.33.xys, f32[72,1024]{1,0:T(8,128)S(1)} %get-tuple-element.34.zc, f32[72,1024]{1,0:T(8,128)S(1)} %get-tuple-element.35.zs, ...), custom_call_target="tpu_custom_call" | custom-call | tf_op jit(solution)/shard_map/pallas_call | solution.py:44
  7.4 1.6 %collective-permute-start = (bf16[640,128]{1,0:T(8,128)(2,1)S(1)}, bf16[640,128]{1,0:T(8,128)(2,1)S(1)}, u32[]{:S(2)}, u32[]{:S(2)}) collective-permute-start(bf16[640,128]{1,0:T(8,128)(2,1)S(1)} %get-tuple-element.38), channel_id=1, source_target_pairs={{0,2},{1,9},{2,0},{3,11},{4,6},{5,13},{6,4},{7,15},{8,10},{9,1},{1... | collective-permute-start | bytes 491528 | tf_op jit(solution)/shard_map/ppermute | solution.py:463
  8.9 0.0 copy-start.2
  8.9 2.1 %shard_map.74 = (bf16[1280,1024]{1,0:T(8,128)(2,1)S(1)}, f32[640,128]{1,0:T(8,128)S(1)}, f32[640,128]{1,0:T(8,128)S(1)}) custom-call(f32[296,1024]{1,0:T(8,128)S(1)} %get-tuple-element.32.xyc, f32[296,1024]{1,0:T(8,128)S(1)} %get-tuple-element.33.xys, f32[72,1024]{1,0:T(8,128)S(1)} %get-tuple-element.34.zc, f32[72,1024]{1,0:T(8,128)S(1)} %get-tuple-element.35.zs, ...), custom_call_target="tpu_custom_call" | custom-call | tf_op jit(solution)/shard_map/pallas_call | solution.py:44
  11.0 0.0 copy-start.5
  11.0 0.0 collective-permute-done.2.b_ref
  11.0 1.6 %collective-permute-start.3 = (bf16[320,128]{1,0:T(8,128)(2,1)S(1)}, bf16[320,128]{1,0:T(8,128)(2,1)S(1)}, u32[]{:S(2)}, u32[]{:S(2)}) collective-permute-start(bf16[320,128]{1,0:T(8,128)(2,1)S(1)} %get-tuple-element.45), channel_id=1, source_target_pairs={{0,8},{1,5},{2,10},{3,7},{4,12},{5,1},{6,14},{7,3},{8,0},{9,13},{1... | collective-permute-start | bytes 245768 | tf_op jit(solution)/shard_map/ppermute | solution.py:463
  12.7 0.1 collective-permute-done.b_ref
  12.8 0.6 %collective-permute-start.1 = (bf16[320,128]{1,0:T(8,128)(2,1)S(1)}, bf16[320,128]{1,0:T(8,128)(2,1)S(1)}, u32[]{:S(2)}, u32[]{:S(2)}) collective-permute-start(bf16[320,128]{1,0:T(8,128)(2,1)S(1)} %get-tuple-element.40), channel_id=1, source_target_pairs={{0,4},{1,3},{2,6},{3,1},{4,0},{5,7},{6,2},{7,5},{8,12},{9,11},{10,... | collective-permute-start | bytes 245768 | tf_op jit(solution)/shard_map/ppermute | solution.py:463
  13.4 2.1 %collective-permute-done.3.b_ref = bf16[320,128]{1,0:T(8,128)(2,1)S(1)} collective-permute-done((bf16[320,128]{1,0:T(8,128)(2,1)S(1)}, bf16[320,128]{1,0:T(8,128)(2,1)S(1)}, u32[]{:S(2)}, u32[]{:S(2)}) %collective-permute-start.3) | collective-permute-done | bytes 81952 | tf_op jit(solution)/shard_map/ppermute | solution.py:463
  15.6 0.7 %collective-permute-start.5 = (bf16[160,128]{1,0:T(8,128)(2,1)S(1)}, bf16[160,128]{1,0:T(8,128)(2,1)S(1)}, u32[]{:S(2)}, u32[]{:S(2)}) collective-permute-start(bf16[160,128]{1,0:T(8,128)(2,1)S(1)} %get-tuple-element.48), channel_id=1, source_target_pairs={{0,2},{1,9},{2,0},{3,11},{4,6},{5,13},{6,4},{7,15},{8,10},{9,1},{1... | collective-permute-start | bytes 122888 | tf_op jit(solution)/shard_map/ppermute | solution.py:463
  16.2 1.0 %collective-permute-done.1.b_ref = bf16[320,128]{1,0:T(8,128)(2,1)S(1)} collective-permute-done((bf16[320,128]{1,0:T(8,128)(2,1)S(1)}, bf16[320,128]{1,0:T(8,128)(2,1)S(1)}, u32[]{:S(2)}, u32[]{:S(2)}) %collective-permute-start.1) | collective-permute-done | bytes 81952 | tf_op jit(solution)/shard_map/ppermute | solution.py:463
  17.3 0.0 copy-start.6
  17.3 1.6 %collective-permute-start.4 = (bf16[160,128]{1,0:T(8,128)(2,1)S(1)}, bf16[160,128]{1,0:T(8,128)(2,1)S(1)}, u32[]{:S(2)}, u32[]{:S(2)}) collective-permute-start(bf16[160,128]{1,0:T(8,128)(2,1)S(1)} %get-tuple-element.47), channel_id=1, source_target_pairs={{0,8},{1,5},{2,10},{3,7},{4,12},{5,1},{6,14},{7,3},{8,0},{9,13},{1... | collective-permute-start | bytes 122888 | tf_op jit(solution)/shard_map/ppermute | solution.py:463
  18.9 0.0 copy-done.2
  19.0 0.0 copy-done.5
  19.0 1.0 %shard_map.82 = (f32[160,128]{1,0:T(8,128)S(1)}, f32[160,128]{1,0:T(8,128)S(1)}) custom-call(s32[3,4096]{1,0:T(4,128)S(1)} %copy-done.5, f32[4096,128]{1,0:T(8,128)S(1)} %bitcast.3), custom_call_target="tpu_custom_call" | custom-call | tf_op jit(solution)/shard_map/pallas_call | solution.py:44
  19.9 0.0 copy-start.4
  20.0 0.0 copy-start.7
  20.0 0.0 copy-start.8
  20.0 0.1 collective-permute-start.7
  20.1 0.0 collective-permute-done.5.refs_3_
  20.1 1.3 %collective-permute-done.4.refs_2_ = bf16[160,128]{1,0:T(8,128)(2,1)S(1)} collective-permute-done((bf16[160,128]{1,0:T(8,128)(2,1)S(1)}, bf16[160,128]{1,0:T(8,128)(2,1)S(1)}, u32[]{:S(2)}, u32[]{:S(2)}) %collective-permute-start.4) | collective-permute-done | bytes 40992 | tf_op jit(solution)/shard_map/ppermute | solution.py:463
  21.4 2.7 %collective-permute-start.6 = (bf16[320,128]{1,0:T(8,128)(2,1)S(1)}, bf16[320,128]{1,0:T(8,128)(2,1)S(1)}, u32[]{:S(2)}, u32[]{:S(2)}) collective-permute-start(bf16[320,128]{1,0:T(8,128)(2,1)S(1)} %get-tuple-element.50), channel_id=1, source_target_pairs={{0,16},{1,17},{2,18},{3,19},{4,20},{5,21},{6,22},{7,23},{8,24},{9,... | collective-permute-start | bytes 245768 | tf_op jit(solution)/shard_map/ppermute | solution.py:463
  24.1 0.0 collective-permute-done.7.refs_1_
  24.1 2.7 %collective-permute-done.6.other_ref = bf16[320,128]{1,0:T(8,128)(2,1)S(1)} collective-permute-done((bf16[320,128]{1,0:T(8,128)(2,1)S(1)}, bf16[320,128]{1,0:T(8,128)(2,1)S(1)}, u32[]{:S(2)}, u32[]{:S(2)}) %collective-permute-start.6) | collective-permute-done | bytes 81952 | tf_op jit(solution)/shard_map/ppermute | solution.py:463
  26.8 0.0 copy-done.6
  26.8 0.3 shard_map.83
  27.1 1.6 %collective-permute-start.8 = (bf16[160,128]{1,0:T(8,128)(2,1)S(1)}, bf16[160,128]{1,0:T(8,128)(2,1)S(1)}, u32[]{:S(2)}, u32[]{:S(2)}) collective-permute-start(bf16[160,128]{1,0:T(8,128)(2,1)S(1)} %get-tuple-element.53.a_ref), channel_id=1, source_target_pairs={{0,8},{1,5},{2,10},{3,7},{4,12},{5,1},{6,14},{7,3},{8,0},{9,13},{1... | collective-permute-start | bytes 122888 | tf_op jit(solution)/shard_map/ppermute | solution.py:463
  28.7 1.9 %collective-permute-start.10 = (bf16[160,128]{1,0:T(8,128)(2,1)S(1)}, bf16[160,128]{1,0:T(8,128)(2,1)S(1)}, u32[]{:S(2)}, u32[]{:S(2)}) collective-permute-start(bf16[160,128]{1,0:T(8,128)(2,1)S(1)} %get-tuple-element.54.a_ref), channel_id=1, source_target_pairs={{0,2},{1,9},{2,0},{3,11},{4,6},{5,13},{6,4},{7,15},{8,10},{9,1},{1... | collective-permute-start | bytes 122888 | tf_op jit(solution)/shard_map/ppermute | solution.py:463
  30.7 0.5 collective-permute-done.8.b_ref
  31.2 0.6 %collective-permute-start.9 = (bf16[320,128]{1,0:T(8,128)(2,1)S(1)}, bf16[320,128]{1,0:T(8,128)(2,1)S(1)}, u32[]{:S(2)}, u32[]{:S(2)}) collective-permute-start(bf16[320,128]{1,0:T(8,128)(2,1)S(1)} %shard_map.84.a_ref), channel_id=1, source_target_pairs={{0,4},{1,3},{2,6},{3,1},{4,0},{5,7},{6,2},{7,5},{8,12},{9,11},{10,... | collective-permute-start | bytes 245768 | tf_op jit(solution)/shard_map/ppermute | solution.py:463
  31.7 1.0 %collective-permute-done.10.b_ref = bf16[160,128]{1,0:T(8,128)(2,1)S(1)} collective-permute-done((bf16[160,128]{1,0:T(8,128)(2,1)S(1)}, bf16[160,128]{1,0:T(8,128)(2,1)S(1)}, u32[]{:S(2)}, u32[]{:S(2)}) %collective-permute-start.10) | collective-permute-done | bytes 40992 | tf_op jit(solution)/shard_map/ppermute | solution.py:463
  32.7 0.6 %collective-permute-start.11 = (bf16[320,128]{1,0:T(8,128)(2,1)S(1)}, bf16[320,128]{1,0:T(8,128)(2,1)S(1)}, u32[]{:S(2)}, u32[]{:S(2)}) collective-permute-start(bf16[320,128]{1,0:T(8,128)(2,1)S(1)} %shard_map.86.a_ref), channel_id=1, source_target_pairs={{0,8},{1,5},{2,10},{3,7},{4,12},{5,1},{6,14},{7,3},{8,0},{9,13},{1... | collective-permute-start | bytes 245768 | tf_op jit(solution)/shard_map/ppermute | solution.py:463
  33.4 2.2 %collective-permute-done.9.b_ref = bf16[320,128]{1,0:T(8,128)(2,1)S(1)} collective-permute-done((bf16[320,128]{1,0:T(8,128)(2,1)S(1)}, bf16[320,128]{1,0:T(8,128)(2,1)S(1)}, u32[]{:S(2)}, u32[]{:S(2)}) %collective-permute-start.9) | collective-permute-done | bytes 81952 | tf_op jit(solution)/shard_map/ppermute | solution.py:463
  35.6 1.7 %collective-permute-start.12 = (bf16[640,128]{1,0:T(8,128)(2,1)S(1)}, bf16[640,128]{1,0:T(8,128)(2,1)S(1)}, u32[]{:S(2)}, u32[]{:S(2)}) collective-permute-start(bf16[640,128]{1,0:T(8,128)(2,1)S(1)} %shard_map.85.refs_0_), channel_id=1, source_target_pairs={{0,2},{1,9},{2,0},{3,11},{4,6},{5,13},{6,4},{7,15},{8,10},{9,1},{1... | collective-permute-start | bytes 491528 | tf_op jit(solution)/shard_map/ppermute | solution.py:463
  37.4 0.1 collective-permute-done.11.b_ref
  37.4 1.0 %collective-permute-start.13 = (bf16[640,128]{1,0:T(8,128)(2,1)S(1)}, bf16[640,128]{1,0:T(8,128)(2,1)S(1)}, u32[]{:S(2)}, u32[]{:S(2)}) collective-permute-start(bf16[640,128]{1,0:T(8,128)(2,1)S(1)} %shard_map.87.refs_1_), channel_id=1, source_target_pairs={{0,4},{1,3},{2,6},{3,1},{4,0},{5,7},{6,2},{7,5},{8,12},{9,11},{10,... | collective-permute-start | bytes 491528 | tf_op jit(solution)/shard_map/ppermute | solution.py:463
  38.4 0.0 copy-done.4
  38.4 0.1 collective-permute-start.14
  38.5 8.1 %collective-permute-done.14.refs_0_ = bf16[560,128]{1,0:T(8,128)(2,1)S(1)} collective-permute-done((bf16[560,128]{1,0:T(8,128)(2,1)S(1)}, bf16[560,128]{1,0:T(8,128)(2,1)S(1)}, u32[]{:S(2)}, u32[]{:S(2)}) %collective-permute-start.14) | collective-permute-done | bytes 143392 | tf_op jit(solution)/shard_map/ppermute | solution.py:481
  46.6 0.0 copy-done.7
  46.6 0.0 copy-done.8
  46.6 3.3 %shard_map.91.short_ref = f32[512,128]{1,0:T(8,128)S(1)} custom-call(f32[3,1024]{1,0:T(4,128)S(1)} %copy-done.4, bf16[1024,128]{1,0:T(8,128)(2,1)S(1)} %copy-done, bf16[128,128]{1,0:T(8,128)(2,1)S(1)} %bitcast.5, bf16[560,128]{1,0:T(8,128)(2,1)S(1)} %collective-permute-done.14.refs_0_, s32[8,8]{1,0:T(8,128)S(1)} %copy-done.8), custom_call_target="tpu_custom_call" | custom-call | tf_op jit(solution)/shard_map/pallas_call | solution.py:44
  50.0 0.9 %shard_map.88.part_ref = f32[1024,128]{1,0:T(8,128)S(1)} custom-call(bf16[1280,1024]{1,0:T(8,128)(2,1)S(1)} %get-tuple-element.36.p_ref, bf16[640,128]{1,0:T(8,128)(2,1)S(1)} %shard_map.85.refs_0_, bf16[640,128]{1,0:T(8,128)(2,1)S(1)} %shard_map.87.refs_1_), custom_call_target="tpu_custom_call" | custom-call | tf_op jit(solution)/shard_map/pallas_call | solution.py:44
  50.9 0.0 collective-permute-done.12.f_ref
  50.9 0.6 %shard_map.89.part_ref = f32[1024,128]{1,0:T(8,128)S(1)} custom-call(f32[1024,128]{1,0:T(8,128)S(1)} %shard_map.88.part_ref, bf16[640,1024]{1,0:T(8,128)(2,1)S(1)} %get-tuple-element.55.p_ref, bf16[640,128]{1,0:T(8,128)(2,1)S(1)} %collective-permute-done.12.f_ref), custom_call_target="tpu_custom_call" | custom-call | tf_op jit(solution)/shard_map/pallas_call | solution.py:44
  51.5 0.0 copy-start.1
  51.5 0.0 collective-permute-done.13.f_ref
  51.5 0.7 %shard_map.92 = (f32[1024,128]{1,0:T(8,128)S(1)}, bf16[1024,128]{1,0:T(8,128)(2,1)S(1)}) custom-call(f32[1024,128]{1,0:T(8,128)S(1)} %shard_map.89.part_ref, bf16[640,1024]{1,0:T(8,128)(2,1)S(1)} %get-tuple-element.56.p_ref, bf16[640,128]{1,0:T(8,128)(2,1)S(1)} %collective-permute-done.13.f_ref, f32[512,128]{1,0:T(8,128)S(1)} %shard_map.91.short_ref), custom_call_target="tpu_custom_call" | custom-call | tf_op jit(solution)/shard_map/pallas_call | solution.py:44
  52.2 0.1 collective-permute-start.15
  52.2 1.5 %collective-permute-done.15.b_ref = bf16[1024,128]{1,0:T(8,128)(2,1)S(1)} collective-permute-done((bf16[1024,128]{1,0:T(8,128)(2,1)S(1)}, bf16[1024,128]{1,0:T(8,128)(2,1)S(1)}, u32[]{:S(2)}, u32[]{:S(2)}) %collective-permute-start.15) | collective-permute-done | bytes 262176 | tf_op jit(solution)/shard_map/ppermute | solution.py:466
  53.8 0.0 copy-done.1
  53.8 0.8 %shard_map.93 = bf16[1024,128]{1,0:T(8,128)(2,1)} custom-call(bf16[1024,128]{1,0:T(8,128)(2,1)S(1)} %copy-done.1, f32[1024,128]{1,0:T(8,128)S(1)} %get-tuple-element.57.a_ref, bf16[1024,128]{1,0:T(8,128)(2,1)S(1)} %collective-permute-done.15.b_ref), custom_call_target="tpu_custom_call" | custom-call | tf_op jit(solution)/shard_map/pallas_call | solution.py:44
  (10 shorter events, 0.2 us)
Async XLA Ops:
  0.0 0.7 %copy-start.3 = (f32[3,1024]{1,0:T(4,128)S(1)}, f32[3,1024]{1,0:T(4,128)}, u32[]{:S(2)}) copy-start(f32[3,1024]{1,0:T(4,128)} %pos_ref.5) | copy-start | bytes 36868
  1.3 1.0 %copy-start = (bf16[1024,128]{1,0:T(8,128)(2,1)S(1)}, bf16[1024,128]{1,0:T(8,128)(2,1)}, u32[]{:S(2)}) copy-start(bf16[1024,128]{1,0:T(8,128)(2,1)} %h_ref.11) | copy-start | bytes 786436
  3.3 7.7 %collective-permute-start.2 = (bf16[640,128]{1,0:T(8,128)(2,1)S(1)}, bf16[640,128]{1,0:T(8,128)(2,1)S(1)}, u32[]{:S(2)}, u32[]{:S(2)}) collective-permute-start(bf16[640,128]{1,0:T(8,128)(2,1)S(1)} %get-tuple-element.43), channel_id=1, source_target_pairs={{0,4},{1,3},{2,6},{3,1},{4,0},{5,7},{6,2},{7,5},{8,12},{9,11},{10,... | collective-permute-start | bytes 491528 | tf_op jit(solution)/shard_map/ppermute | solution.py:463
  7.4 5.4 %collective-permute-start = (bf16[640,128]{1,0:T(8,128)(2,1)S(1)}, bf16[640,128]{1,0:T(8,128)(2,1)S(1)}, u32[]{:S(2)}, u32[]{:S(2)}) collective-permute-start(bf16[640,128]{1,0:T(8,128)(2,1)S(1)} %get-tuple-element.38), channel_id=1, source_target_pairs={{0,2},{1,9},{2,0},{3,11},{4,6},{5,13},{6,4},{7,15},{8,10},{9,1},{1... | collective-permute-start | bytes 491528 | tf_op jit(solution)/shard_map/ppermute | solution.py:463
  8.9 10.0 %copy-start.2 = (f32[1,4096,128]{2,1,0:T(8,128)S(1)}, f32[1,4096,128]{2,1,0:T(8,128)}, u32[]{:S(2)}) copy-start(f32[1,4096,128]{2,1,0:T(8,128)} %param.13) | copy-start | bytes 6291460
  11.0 8.0 %copy-start.5 = (s32[3,4096]{1,0:T(4,128)S(1)}, s32[3,4096]{1,0:T(4,128)}, u32[]{:S(2)}) copy-start(s32[3,4096]{1,0:T(4,128)} %wave_ref.1) | copy-start | bytes 147460
  11.0 4.5 %collective-permute-start.3 = (bf16[320,128]{1,0:T(8,128)(2,1)S(1)}, bf16[320,128]{1,0:T(8,128)(2,1)S(1)}, u32[]{:S(2)}, u32[]{:S(2)}) collective-permute-start(bf16[320,128]{1,0:T(8,128)(2,1)S(1)} %get-tuple-element.45), channel_id=1, source_target_pairs={{0,8},{1,5},{2,10},{3,7},{4,12},{5,1},{6,14},{7,3},{8,0},{9,13},{1... | collective-permute-start | bytes 245768 | tf_op jit(solution)/shard_map/ppermute | solution.py:463
  12.8 4.5 %collective-permute-start.1 = (bf16[320,128]{1,0:T(8,128)(2,1)S(1)}, bf16[320,128]{1,0:T(8,128)(2,1)S(1)}, u32[]{:S(2)}, u32[]{:S(2)}) collective-permute-start(bf16[320,128]{1,0:T(8,128)(2,1)S(1)} %get-tuple-element.40), channel_id=1, source_target_pairs={{0,4},{1,3},{2,6},{3,1},{4,0},{5,7},{6,2},{7,5},{8,12},{9,11},{10,... | collective-permute-start | bytes 245768 | tf_op jit(solution)/shard_map/ppermute | solution.py:463
  15.6 4.5 %collective-permute-start.5 = (bf16[160,128]{1,0:T(8,128)(2,1)S(1)}, bf16[160,128]{1,0:T(8,128)(2,1)S(1)}, u32[]{:S(2)}, u32[]{:S(2)}) collective-permute-start(bf16[160,128]{1,0:T(8,128)(2,1)S(1)} %get-tuple-element.48), channel_id=1, source_target_pairs={{0,2},{1,9},{2,0},{3,11},{4,6},{5,13},{6,4},{7,15},{8,10},{9,1},{1... | collective-permute-start | bytes 122888 | tf_op jit(solution)/shard_map/ppermute | solution.py:463
  17.3 9.5 %copy-start.6 = (f32[1,128,128]{2,1,0:T(8,128)S(1)}, f32[1,128,128]{2,1,0:T(8,128)}, u32[]{:S(2)}) copy-start(f32[1,128,128]{2,1,0:T(8,128)} %param.12) | copy-start | bytes 196612
  17.3 4.1 %collective-permute-start.4 = (bf16[160,128]{1,0:T(8,128)(2,1)S(1)}, bf16[160,128]{1,0:T(8,128)(2,1)S(1)}, u32[]{:S(2)}, u32[]{:S(2)}) collective-permute-start(bf16[160,128]{1,0:T(8,128)(2,1)S(1)} %get-tuple-element.47), channel_id=1, source_target_pairs={{0,8},{1,5},{2,10},{3,7},{4,12},{5,1},{6,14},{7,3},{8,0},{9,13},{1... | collective-permute-start | bytes 122888 | tf_op jit(solution)/shard_map/ppermute | solution.py:463
  19.9 18.5 %copy-start.4 = (f32[3,1024]{1,0:T(4,128)S(1)}, f32[3,1024]{1,0:T(4,128)}, u32[]{:S(2)}) copy-start(f32[3,1024]{1,0:T(4,128)} %pos_ref.5) | copy-start | bytes 36868
  20.0 26.7 %copy-start.7 = (bf16[1,128,128]{2,1,0:T(8,128)(2,1)S(1)}, bf16[1,128,128]{2,1,0:T(8,128)(2,1)}, u32[]{:S(2)}) copy-start(bf16[1,128,128]{2,1,0:T(8,128)(2,1)} %param.11) | copy-start | bytes 98308
  20.0 26.7 %copy-start.8 = (s32[8,8]{1,0:T(8,128)S(1)}, s32[8,8]{1,0:T(8,128)}, u32[]{:S(2)}) copy-start(s32[8,8]{1,0:T(8,128)} %refs_1_.1) | copy-start | bytes 772
  20.0 4.1 %collective-permute-start.7 = (f32[160,128]{1,0:T(8,128)S(1)}, f32[160,128]{1,0:T(8,128)S(1)}, u32[]{:S(2)}, u32[]{:S(2)}) collective-permute-start(f32[160,128]{1,0:T(8,128)S(1)} %get-tuple-element.52), channel_id=1, source_target_pairs={{0,1},{1,0},{2,3},{3,2},{4,5},{5,4},{6,7},{7,6},{8,9},{9,8},{10,11... | collective-permute-start | bytes 245768 | tf_op jit(solution)/shard_map/ppermute | solution.py:466
  21.4 5.4 %collective-permute-start.6 = (bf16[320,128]{1,0:T(8,128)(2,1)S(1)}, bf16[320,128]{1,0:T(8,128)(2,1)S(1)}, u32[]{:S(2)}, u32[]{:S(2)}) collective-permute-start(bf16[320,128]{1,0:T(8,128)(2,1)S(1)} %get-tuple-element.50), channel_id=1, source_target_pairs={{0,16},{1,17},{2,18},{3,19},{4,20},{5,21},{6,22},{7,23},{8,24},{9,... | collective-permute-start | bytes 245768 | tf_op jit(solution)/shard_map/ppermute | solution.py:463
  27.1 4.1 %collective-permute-start.8 = (bf16[160,128]{1,0:T(8,128)(2,1)S(1)}, bf16[160,128]{1,0:T(8,128)(2,1)S(1)}, u32[]{:S(2)}, u32[]{:S(2)}) collective-permute-start(bf16[160,128]{1,0:T(8,128)(2,1)S(1)} %get-tuple-element.53.a_ref), channel_id=1, source_target_pairs={{0,8},{1,5},{2,10},{3,7},{4,12},{5,1},{6,14},{7,3},{8,0},{9,13},{1... | collective-permute-start | bytes 122888 | tf_op jit(solution)/shard_map/ppermute | solution.py:463
  28.7 4.0 %collective-permute-start.10 = (bf16[160,128]{1,0:T(8,128)(2,1)S(1)}, bf16[160,128]{1,0:T(8,128)(2,1)S(1)}, u32[]{:S(2)}, u32[]{:S(2)}) collective-permute-start(bf16[160,128]{1,0:T(8,128)(2,1)S(1)} %get-tuple-element.54.a_ref), channel_id=1, source_target_pairs={{0,2},{1,9},{2,0},{3,11},{4,6},{5,13},{6,4},{7,15},{8,10},{9,1},{1... | collective-permute-start | bytes 122888 | tf_op jit(solution)/shard_map/ppermute | solution.py:463
  31.2 4.4 %collective-permute-start.9 = (bf16[320,128]{1,0:T(8,128)(2,1)S(1)}, bf16[320,128]{1,0:T(8,128)(2,1)S(1)}, u32[]{:S(2)}, u32[]{:S(2)}) collective-permute-start(bf16[320,128]{1,0:T(8,128)(2,1)S(1)} %shard_map.84.a_ref), channel_id=1, source_target_pairs={{0,4},{1,3},{2,6},{3,1},{4,0},{5,7},{6,2},{7,5},{8,12},{9,11},{10,... | collective-permute-start | bytes 245768 | tf_op jit(solution)/shard_map/ppermute | solution.py:463
  32.7 4.7 %collective-permute-start.11 = (bf16[320,128]{1,0:T(8,128)(2,1)S(1)}, bf16[320,128]{1,0:T(8,128)(2,1)S(1)}, u32[]{:S(2)}, u32[]{:S(2)}) collective-permute-start(bf16[320,128]{1,0:T(8,128)(2,1)S(1)} %shard_map.86.a_ref), channel_id=1, source_target_pairs={{0,8},{1,5},{2,10},{3,7},{4,12},{5,1},{6,14},{7,3},{8,0},{9,13},{1... | collective-permute-start | bytes 245768 | tf_op jit(solution)/shard_map/ppermute | solution.py:463
  35.6 15.3 %collective-permute-start.12 = (bf16[640,128]{1,0:T(8,128)(2,1)S(1)}, bf16[640,128]{1,0:T(8,128)(2,1)S(1)}, u32[]{:S(2)}, u32[]{:S(2)}) collective-permute-start(bf16[640,128]{1,0:T(8,128)(2,1)S(1)} %shard_map.85.refs_0_), channel_id=1, source_target_pairs={{0,2},{1,9},{2,0},{3,11},{4,6},{5,13},{6,4},{7,15},{8,10},{9,1},{1... | collective-permute-start | bytes 491528 | tf_op jit(solution)/shard_map/ppermute | solution.py:463
  37.4 14.0 %collective-permute-start.13 = (bf16[640,128]{1,0:T(8,128)(2,1)S(1)}, bf16[640,128]{1,0:T(8,128)(2,1)S(1)}, u32[]{:S(2)}, u32[]{:S(2)}) collective-permute-start(bf16[640,128]{1,0:T(8,128)(2,1)S(1)} %shard_map.87.refs_1_), channel_id=1, source_target_pairs={{0,4},{1,3},{2,6},{3,1},{4,0},{5,7},{6,2},{7,5},{8,12},{9,11},{10,... | collective-permute-start | bytes 491528 | tf_op jit(solution)/shard_map/ppermute | solution.py:463
  38.4 8.2 %collective-permute-start.14 = (bf16[560,128]{1,0:T(8,128)(2,1)S(1)}, bf16[560,128]{1,0:T(8,128)(2,1)S(1)}, u32[]{:S(2)}, u32[]{:S(2)}) collective-permute-start(bf16[560,128]{1,0:T(8,128)(2,1)S(1)} %shard_map.90), channel_id=1, source_target_pairs={{0,31},{1,2},{2,1},{3,4},{4,3},{5,6},{6,5},{7,8},{8,7},{9,10},{10,... | collective-permute-start | bytes 430088 | tf_op jit(solution)/shard_map/ppermute | solution.py:481
  51.5 2.3 %copy-start.1 = (bf16[1024,128]{1,0:T(8,128)(2,1)S(1)}, bf16[1024,128]{1,0:T(8,128)(2,1)}, u32[]{:S(2)}) copy-start(bf16[1024,128]{1,0:T(8,128)(2,1)} %h_ref.11) | copy-start | bytes 786436
  52.2 1.6 %collective-permute-start.15 = (bf16[1024,128]{1,0:T(8,128)(2,1)S(1)}, bf16[1024,128]{1,0:T(8,128)(2,1)S(1)}, u32[]{:S(2)}, u32[]{:S(2)}) collective-permute-start(bf16[1024,128]{1,0:T(8,128)(2,1)S(1)} %get-tuple-element.58), channel_id=1, source_target_pairs={{0,1},{1,0},{2,3},{3,2},{4,5},{5,4},{6,7},{7,6},{8,9},{9,8},{10,11... | collective-permute-start | bytes 786440 | tf_op jit(solution)/shard_map/ppermute | solution.py:466
where the time goes:
time: 54.8 us; the launch traced here: 54.6 us
  waiting for transfers between devices  20.7 us (38%)
  starting transfers between devices  19.5 us (36%)
  Pallas kernels  12.4 us (23%)
  local copies, waits for them, and re-layouts  1.7 us (3%)
    ppermute x13, starting transfers between devices, swap(): return lax.ppermute(x, ('dom', 'wav'), pairs)  19.3 us
    pallas_call x21, Pallas kernels, call(): pl.pallas_call(body, in_specs=specs, out_specs=spec if single else [spec]...  12.4 us
    ppermute x13, waiting for transfers between devices, swap(): return lax.ppermute(x, ('dom', 'wav'), pairs)  11.1 us
    ppermute x1, waiting for transfers between devices, local(): halos = [lax.ppermute(packed, ('dom', 'wav'), chain)]  8.11 us
    unnamed x18, local copies, waits for them, and re-layouts  1.7 us
    ppermute x2, waiting for transfers between devices, swap_wav(): return lax.ppermute(x, 'wav', [(w, w ^ mask) for w in range(wavs)])  1.52 us
  transfers between devices with their start and end apart: 16, of which 11 were waited for; matrix products, arithmetic and copies ran while one was open for 0% of the time, Pallas kernels for 17%

commit v1 on v0

--- a/solution.py
+++ b/solution.py
@@ -17,6 +17,8 @@
 
 TWO_PI = 2.0 * math.pi
 KERNEL_DECAY = 12.0
+DECAY_LOG2 = -KERNEL_DECAY * math.log2(math.e)
+SPLIT = 64
 PAIR_SCALE = 1.0 / 16.0
 
 TILE = 8
@@ -37,9 +39,14 @@
     return pltpu.with_memory_space_constraint(array, VMEM)
 
 
-def call(body, out, *args, smem=(), scratch=(), limit=16):
+def in_hbm(array):
+    return pltpu.with_memory_space_constraint(array, pltpu.HBM)
+
+
+def call(body, out, *args, smem=(), hbm=(), scratch=(), limit=16):
     spec = pl.BlockSpec(memory_space=VMEM)
     specs = [spec] * len(args) + [pl.BlockSpec(memory_space=pltpu.SMEM)] * len(smem)
+    specs += [pl.BlockSpec(memory_space=pltpu.HBM)] * len(hbm)
     single = not isinstance(out, (list, tuple))
     return pl.pallas_call(
         body,
@@ -48,11 +55,11 @@
         out_shape=out,
         scratch_shapes=list(scratch),
         compiler_params=pltpu.CompilerParams(vmem_limit_bytes=limit << 20),
-    )(*[in_vmem(a) for a in args], *smem)
+    )(*[in_vmem(a) for a in args], *smem, *[in_hbm(a) for a in hbm])
 
 
 DIVIDE = -(-(1 << 16) // Q_TILES)
-assert all((v * DIVIDE) >> 16 == v // Q_TILES for v in range(ALL_TILES))
+assert all((v * DIVIDE) >> 16 == v // Q_TILES for v in range(FIRST_TILE + ALL_TILES))
 
 
 class Layout:
@@ -87,12 +94,9 @@
 
 
 def tile_place(tile):
-    tile = jnp.minimum(tile, ALL_TILES - 1)
-    later = tile - ZERO_TILES
-    first = later < 0
-    plane = (jnp.maximum(later, 0) * DIVIDE) >> 16
-    n2 = jnp.where(first, 0, 1 + plane)
-    return n2, jnp.where(first, FIRST_TILE + tile, later - plane * Q_TILES)
+    tile = jnp.minimum(tile, ALL_TILES - 1) + FIRST_TILE
+    n2 = (tile * DIVIDE) >> 16
+    return n2, tile - n2 * Q_TILES
 
 
 def times(a, b):
@@ -144,8 +148,8 @@
     rows = group * lay.slice_rows
     feats = h_ref[...]
 
-    def chunk(step, carry):
-        start = pl.multiple_of(step * rows, rows)
+    for step in range(count // group):
+        start = p_at + step * rows
         for part in range(group):
             base = lay.first_tile(wav, chain, low + step * group + part)
             for i in range(lay.tiles):
@@ -153,20 +157,34 @@
                 q_at = pl.ds(pl.multiple_of(qt * TILE, TILE), TILE)
                 z_at = pl.ds(pl.multiple_of(n2 * TILE, TILE), TILE)
                 c, s = times((xyc_ref[q_at, :], xys_ref[q_at, :]), (zc_ref[z_at, :], zs_ref[z_at, :]))
-                at = p_at + start + (part * lay.tiles + i) * 2 * TILE
-                at = pl.ds(pl.multiple_of(at, 2 * TILE), 2 * TILE)
-                p_ref[at, :] = jnp.concatenate([c, s], axis=0).astype(BF16)
-        here = pl.ds(pl.multiple_of(p_at + start, rows), rows)
-        put(pl.ds(start, rows), jnp.dot(p_ref[here, :], feats, preferred_element_type=F32))
-        return carry
-
-    lax.fori_loop(0, count // group, chunk, 0)
-
-
-def phase_tables(positions):
+                at = start + (part * lay.tiles + i) * 2 * TILE
+                p_ref[at : at + 2 * TILE, :] = jnp.concatenate([c, s], axis=0).astype(BF16)
+        here = slice(start, start + rows)
+        at = slice(step * rows, (step + 1) * rows)
+        put(at, jnp.dot(p_ref[here, :], feats, preferred_element_type=F32))
+
+
+def phase_tables(positions, features):
     atoms = positions.shape[1]
     table = [(Q_ROWS, atoms)] * 2 + [((TOP + 1) * TILE, atoms)] * 2
-    return call(fill_tables, [VMEM(shape, F32) for shape in table], positions)
+
+    def body(pos_hbm, h_hbm, *refs):
+        *table_refs, pos_ref, h_ref, sems = refs
+        bring_pos = pltpu.make_async_copy(pos_hbm, pos_ref, sems.at[0])
+        bring_h = pltpu.make_async_copy(h_hbm, h_ref, sems.at[1])
+        bring_pos.start()
+        bring_h.start()
+        bring_pos.wait()
+        fill_tables(pos_ref, *table_refs)
+        bring_h.wait()
+
+    out = [VMEM(shape, F32) for shape in table]
+    out += [VMEM(positions.shape, F32), VMEM(features.shape, BF16)]
+    *tables, pos, h = call(
+        body, out, hbm=[positions, features],
+        scratch=[pltpu.SemaphoreType.DMA((2,))],
+    )
+    return tables, pos, h
 
 
 def spectrum_upper(lay, chain, scale, tables, features):
@@ -378,19 +396,23 @@
                     outside = own + jnp.where(ext < HALO_BLK, ext, ext - HALO_BLK - own)
                 sender = jnp.where(inside, ext - HALO_BLK, outside)
                 sent = at_ref[sender]
-                distance = None
-                for axis in range(3):
-                    delta = columns[:, axis : axis + 1] - sent[axis : axis + 1, :]
-                    delta = delta - jnp.floor(delta + 0.5)
-                    square = delta * delta
-                    distance = square if distance is None else distance + square
-                kernel = jnp.exp(-KERNEL_DECAY * distance).astype(BF16)
+                parts = []
+                for low in range(0, BLOCK, SPLIT):
+                    distance = None
+                    for axis in range(3):
+                        here = columns[low : low + SPLIT, axis : axis + 1]
+                        delta = here - sent[axis : axis + 1, :]
+                        delta = delta - jnp.round(delta)
+                        square = delta * delta
+                        distance = square if distance is None else distance + square
+                    parts.append(jnp.exp2(distance * DECAY_LOG2).astype(BF16))
+                kernel = jnp.concatenate(parts, axis=0)
                 rows = pl.ds(pl.multiple_of(sender * BLOCK, BLOCK), BLOCK)
                 total = total + jnp.dot(kernel, val_ref[rows, :], preferred_element_type=F32)
             out_ref[pl.ds(pl.multiple_of(b * BLOCK, BLOCK), BLOCK), :] = total * PAIR_SCALE
             return carry
 
-        lax.fori_loop(0, share, block, 0)
+        lax.fori_loop(0, share, block, 0, unroll=True)
 
     return call(
         body, VMEM((share * BLOCK, channels), F32), positions, features, weight,
@@ -466,7 +488,7 @@
         return lax.ppermute(x, "wav", [(w, w ^ mask) for w in range(wavs)])
 
     each = range(CHAINS)
-    tables = phase_tables(positions)
+    tables, positions, features = phase_tables(positions, features)
     phases_up, arrived = [], []
     for c in each:
         phases, leaving = spectrum_upper(lay, c, inv_atoms, tables, features)

time: 54.8 us -> 52.8 us (0.964)
  starting transfers between devices: 19.5 us -> 22.3 us
  Pallas kernels: 12.4 us -> 10.5 us
  local copies, waits for them, and re-layouts: 1.7 us -> 0.03 us
  waiting for transfers between devices: 20.7 us -> 19.5 us
    ppermute x13, starting transfers between devices: 19.3 us -> 22.1 us  [swap(): return lax.ppermute(x, ('dom', 'wav'), pairs)]
    pallas_call x21, Pallas kernels: 12.4 us -> 10.5 us  [call(): pl.pallas_call(body, in_specs=specs, out_specs=spec if single else [spec]...]
    unnamed x18 -> x10, local copies, waits for them, and re-layouts: 1.7 us -> 0.03 us
    ppermute x13, waiting for transfers between devices: 11.1 us -> 9.88 us  [swap(): return lax.ppermute(x, ('dom', 'wav'), pairs)]
  transfers between devices with their start and end apart: 16 -> 16, of which waited for: 11 -> 10; matrix products, arithmetic and copies ran while one was open for 0% -> 0% of each run, Pallas kernels for 17% -> 13%
where the time goes in v1:
time: 52.8 us; the launch traced here: 52.5 us
  starting transfers between devices  22.3 us (42%)
  waiting for transfers between devices  19.5 us (37%)
  Pallas kernels  10.5 us (20%)
    ppermute x13, starting transfers between devices, swap(): return lax.ppermute(x, ('dom', 'wav'), pairs)  22.1 us
    pallas_call x21, Pallas kernels, call(): pl.pallas_call(body, in_specs=specs, out_specs=spec if single else [spec]...  10.5 us
    ppermute x13, waiting for transfers between devices, swap(): return lax.ppermute(x, ('dom', 'wav'), pairs)  9.88 us
    ppermute x1, waiting for transfers between devices, local(): halos = [lax.ppermute(packed, ('dom', 'wav'), chain)]  8.11 us
    ppermute x2, waiting for transfers between devices, swap_wav(): return lax.ppermute(x, 'wav', [(w, w ^ mask) for w in range(wavs)])  1.52 us
  transfers between devices with their start and end apart: 16, of which 10 were waited for; matrix products, arithmetic and copies ran while one was open for 0% of the time, Pallas kernels for 13%

profile of v1, /device:TPU:0, one launch (start us, length us, event | category | flops | bytes accessed | tf_op | source)
XLA Modules:
  0.0 52.5 jit_solution(9842418075571144949)
XLA Ops:
  0.0 1.3 %shard_map.73 = (f32[296,1024]{1,0:T(8,128)S(1)}, f32[296,1024]{1,0:T(8,128)S(1)}, f32[72,1024]{1,0:T(8,128)S(1)}, f32[72,1024]{1,0:T(8,128)S(1)}, f32[3,1024]{1,0:T(4,128)S(1)}, /*index=5*/bf16[1024,128]{1,0:T(8,128)(2,1)S(1)}) custom-call(f32[3,1024]{1,0:T(4,128)} %pos_hbm.1, bf16[1024,128]{1,0:T(8,128)(2,1)} %h_hbm.1), custom_call_target="tpu_custom_call" | custom-call | tf_op jit(solution)/shard_map/pallas_call | solution.py:51
  1.3 0.7 %shard_map.78 = (bf16[640,1024]{1,0:T(8,128)(2,1)S(1)}, bf16[640,128]{1,0:T(8,128)(2,1)S(1)}) custom-call(f32[296,1024]{1,0:T(8,128)S(1)} %get-tuple-element.35.xyc, f32[296,1024]{1,0:T(8,128)S(1)} %get-tuple-element.36.xys, f32[72,1024]{1,0:T(8,128)S(1)} %get-tuple-element.37.zc, f32[72,1024]{1,0:T(8,128)S(1)} %get-tuple-element.38.zs, ...), custom_call_target="tpu_custom_call" | custom-call | tf_op jit(solution)/shard_map/pallas_call | solution.py:51
  2.0 3.1 %collective-permute-start.2 = (bf16[640,128]{1,0:T(8,128)(2,1)S(1)}, bf16[640,128]{1,0:T(8,128)(2,1)S(1)}, u32[]{:S(2)}, u32[]{:S(2)}) collective-permute-start(bf16[640,128]{1,0:T(8,128)(2,1)S(1)} %get-tuple-element.46), channel_id=1, source_target_pairs={{0,4},{1,3},{2,6},{3,1},{4,0},{5,7},{6,2},{7,5},{8,12},{9,11},{10,... | collective-permute-start | bytes 491528 | tf_op jit(solution)/shard_map/ppermute | solution.py:485
  5.1 0.7 %shard_map.75 = (bf16[640,1024]{1,0:T(8,128)(2,1)S(1)}, bf16[640,128]{1,0:T(8,128)(2,1)S(1)}) custom-call(f32[296,1024]{1,0:T(8,128)S(1)} %get-tuple-element.35.xyc, f32[296,1024]{1,0:T(8,128)S(1)} %get-tuple-element.36.xys, f32[72,1024]{1,0:T(8,128)S(1)} %get-tuple-element.37.zc, f32[72,1024]{1,0:T(8,128)S(1)} %get-tuple-element.38.zs, ...), custom_call_target="tpu_custom_call" | custom-call | tf_op jit(solution)/shard_map/pallas_call | solution.py:51
  5.8 1.6 %collective-permute-start = (bf16[640,128]{1,0:T(8,128)(2,1)S(1)}, bf16[640,128]{1,0:T(8,128)(2,1)S(1)}, u32[]{:S(2)}, u32[]{:S(2)}) collective-permute-start(bf16[640,128]{1,0:T(8,128)(2,1)S(1)} %get-tuple-element.41), channel_id=1, source_target_pairs={{0,2},{1,9},{2,0},{3,11},{4,6},{5,13},{6,4},{7,15},{8,10},{9,1},{1... | collective-permute-start | bytes 491528 | tf_op jit(solution)/shard_map/ppermute | solution.py:485
  7.3 0.0 copy-start
  7.3 1.2 %shard_map.74 = (bf16[1280,1024]{1,0:T(8,128)(2,1)S(1)}, f32[640,128]{1,0:T(8,128)S(1)}, f32[640,128]{1,0:T(8,128)S(1)}) custom-call(f32[296,1024]{1,0:T(8,128)S(1)} %get-tuple-element.35.xyc, f32[296,1024]{1,0:T(8,128)S(1)} %get-tuple-element.36.xys, f32[72,1024]{1,0:T(8,128)S(1)} %get-tuple-element.37.zc, f32[72,1024]{1,0:T(8,128)S(1)} %get-tuple-element.38.zs, ...), custom_call_target="tpu_custom_call" | custom-call | tf_op jit(solution)/shard_map/pallas_call | solution.py:51
  8.6 0.0 copy-start.1
  8.6 0.0 collective-permute-done.2.b_ref
  8.6 1.9 %collective-permute-start.3 = (bf16[320,128]{1,0:T(8,128)(2,1)S(1)}, bf16[320,128]{1,0:T(8,128)(2,1)S(1)}, u32[]{:S(2)}, u32[]{:S(2)}) collective-permute-start(bf16[320,128]{1,0:T(8,128)(2,1)S(1)} %get-tuple-element.48), channel_id=1, source_target_pairs={{0,8},{1,5},{2,10},{3,7},{4,12},{5,1},{6,14},{7,3},{8,0},{9,13},{1... | collective-permute-start | bytes 245768 | tf_op jit(solution)/shard_map/ppermute | solution.py:485
  10.5 0.6 %collective-permute-done.b_ref = bf16[640,128]{1,0:T(8,128)(2,1)S(1)} collective-permute-done((bf16[640,128]{1,0:T(8,128)(2,1)S(1)}, bf16[640,128]{1,0:T(8,128)(2,1)S(1)}, u32[]{:S(2)}, u32[]{:S(2)}) %collective-permute-start) | collective-permute-done | bytes 163872 | tf_op jit(solution)/shard_map/ppermute | solution.py:485
  11.2 1.0 %collective-permute-start.1 = (bf16[320,128]{1,0:T(8,128)(2,1)S(1)}, bf16[320,128]{1,0:T(8,128)(2,1)S(1)}, u32[]{:S(2)}, u32[]{:S(2)}) collective-permute-start(bf16[320,128]{1,0:T(8,128)(2,1)S(1)} %get-tuple-element.43), channel_id=1, source_target_pairs={{0,4},{1,3},{2,6},{3,1},{4,0},{5,7},{6,2},{7,5},{8,12},{9,11},{10,... | collective-permute-start | bytes 245768 | tf_op jit(solution)/shard_map/ppermute | solution.py:485
  12.2 1.0 %collective-permute-done.3.b_ref = bf16[320,128]{1,0:T(8,128)(2,1)S(1)} collective-permute-done((bf16[320,128]{1,0:T(8,128)(2,1)S(1)}, bf16[320,128]{1,0:T(8,128)(2,1)S(1)}, u32[]{:S(2)}, u32[]{:S(2)}) %collective-permute-start.3) | collective-permute-done | bytes 81952 | tf_op jit(solution)/shard_map/ppermute | solution.py:485
  13.2 1.8 %collective-permute-start.5 = (bf16[160,128]{1,0:T(8,128)(2,1)S(1)}, bf16[160,128]{1,0:T(8,128)(2,1)S(1)}, u32[]{:S(2)}, u32[]{:S(2)}) collective-permute-start(bf16[160,128]{1,0:T(8,128)(2,1)S(1)} %get-tuple-element.51), channel_id=1, source_target_pairs={{0,2},{1,9},{2,0},{3,11},{4,6},{5,13},{6,4},{7,15},{8,10},{9,1},{1... | collective-permute-start | bytes 122888 | tf_op jit(solution)/shard_map/ppermute | solution.py:485
  15.0 0.7 %collective-permute-done.1.b_ref = bf16[320,128]{1,0:T(8,128)(2,1)S(1)} collective-permute-done((bf16[320,128]{1,0:T(8,128)(2,1)S(1)}, bf16[320,128]{1,0:T(8,128)(2,1)S(1)}, u32[]{:S(2)}, u32[]{:S(2)}) %collective-permute-start.1) | collective-permute-done | bytes 81952 | tf_op jit(solution)/shard_map/ppermute | solution.py:485
  15.7 0.0 copy-start.2
  15.7 1.6 %collective-permute-start.4 = (bf16[160,128]{1,0:T(8,128)(2,1)S(1)}, bf16[160,128]{1,0:T(8,128)(2,1)S(1)}, u32[]{:S(2)}, u32[]{:S(2)}) collective-permute-start(bf16[160,128]{1,0:T(8,128)(2,1)S(1)} %get-tuple-element.50), channel_id=1, source_target_pairs={{0,8},{1,5},{2,10},{3,7},{4,12},{5,1},{6,14},{7,3},{8,0},{9,13},{1... | collective-permute-start | bytes 122888 | tf_op jit(solution)/shard_map/ppermute | solution.py:485
  17.4 0.0 copy-done
  17.4 0.0 copy-done.1
  17.4 0.9 %shard_map.82 = (f32[160,128]{1,0:T(8,128)S(1)}, f32[160,128]{1,0:T(8,128)S(1)}) custom-call(s32[3,4096]{1,0:T(4,128)S(1)} %copy-done.1, f32[4096,128]{1,0:T(8,128)S(1)} %bitcast.3), custom_call_target="tpu_custom_call" | custom-call | tf_op jit(solution)/shard_map/pallas_call | solution.py:51
  18.3 0.0 copy-start.3
  18.3 0.0 copy-start.4
  18.3 0.1 collective-permute-start.7
  18.4 0.0 collective-permute-done.5.refs_3_
  18.4 1.4 %collective-permute-done.4.refs_2_ = bf16[160,128]{1,0:T(8,128)(2,1)S(1)} collective-permute-done((bf16[160,128]{1,0:T(8,128)(2,1)S(1)}, bf16[160,128]{1,0:T(8,128)(2,1)S(1)}, u32[]{:S(2)}, u32[]{:S(2)}) %collective-permute-start.4) | collective-permute-done | bytes 40992 | tf_op jit(solution)/shard_map/ppermute | solution.py:485
  19.8 2.7 %collective-permute-start.6 = (bf16[320,128]{1,0:T(8,128)(2,1)S(1)}, bf16[320,128]{1,0:T(8,128)(2,1)S(1)}, u32[]{:S(2)}, u32[]{:S(2)}) collective-permute-start(bf16[320,128]{1,0:T(8,128)(2,1)S(1)} %get-tuple-element.53), channel_id=1, source_target_pairs={{0,16},{1,17},{2,18},{3,19},{4,20},{5,21},{6,22},{7,23},{8,24},{9,... | collective-permute-start | bytes 245768 | tf_op jit(solution)/shard_map/ppermute | solution.py:485
  22.5 0.0 collective-permute-done.7.refs_1_
  22.5 2.7 %collective-permute-done.6.other_ref = bf16[320,128]{1,0:T(8,128)(2,1)S(1)} collective-permute-done((bf16[320,128]{1,0:T(8,128)(2,1)S(1)}, bf16[320,128]{1,0:T(8,128)(2,1)S(1)}, u32[]{:S(2)}, u32[]{:S(2)}) %collective-permute-start.6) | collective-permute-done | bytes 81952 | tf_op jit(solution)/shard_map/ppermute | solution.py:485
  25.2 0.0 copy-done.2
  25.2 0.3 shard_map.83
  25.5 1.6 %collective-permute-start.8 = (bf16[160,128]{1,0:T(8,128)(2,1)S(1)}, bf16[160,128]{1,0:T(8,128)(2,1)S(1)}, u32[]{:S(2)}, u32[]{:S(2)}) collective-permute-start(bf16[160,128]{1,0:T(8,128)(2,1)S(1)} %get-tuple-element.56.a_ref), channel_id=1, source_target_pairs={{0,8},{1,5},{2,10},{3,7},{4,12},{5,1},{6,14},{7,3},{8,0},{9,13},{1... | collective-permute-start | bytes 122888 | tf_op jit(solution)/shard_map/ppermute | solution.py:485
  27.2 1.6 %collective-permute-start.10 = (bf16[160,128]{1,0:T(8,128)(2,1)S(1)}, bf16[160,128]{1,0:T(8,128)(2,1)S(1)}, u32[]{:S(2)}, u32[]{:S(2)}) collective-permute-start(bf16[160,128]{1,0:T(8,128)(2,1)S(1)} %get-tuple-element.57.a_ref), channel_id=1, source_target_pairs={{0,2},{1,9},{2,0},{3,11},{4,6},{5,13},{6,4},{7,15},{8,10},{9,1},{1... | collective-permute-start | bytes 122888 | tf_op jit(solution)/shard_map/ppermute | solution.py:485
  28.8 0.8 %collective-permute-done.8.b_ref = bf16[160,128]{1,0:T(8,128)(2,1)S(1)} collective-permute-done((bf16[160,128]{1,0:T(8,128)(2,1)S(1)}, bf16[160,128]{1,0:T(8,128)(2,1)S(1)}, u32[]{:S(2)}, u32[]{:S(2)}) %collective-permute-start.8) | collective-permute-done | bytes 40992 | tf_op jit(solution)/shard_map/ppermute | solution.py:485
  29.6 0.9 %collective-permute-start.9 = (bf16[320,128]{1,0:T(8,128)(2,1)S(1)}, bf16[320,128]{1,0:T(8,128)(2,1)S(1)}, u32[]{:S(2)}, u32[]{:S(2)}) collective-permute-start(bf16[320,128]{1,0:T(8,128)(2,1)S(1)} %shard_map.84.a_ref), channel_id=1, source_target_pairs={{0,4},{1,3},{2,6},{3,1},{4,0},{5,7},{6,2},{7,5},{8,12},{9,11},{10,... | collective-permute-start | bytes 245768 | tf_op jit(solution)/shard_map/ppermute | solution.py:485
  30.5 0.7 %collective-permute-done.10.b_ref = bf16[160,128]{1,0:T(8,128)(2,1)S(1)} collective-permute-done((bf16[160,128]{1,0:T(8,128)(2,1)S(1)}, bf16[160,128]{1,0:T(8,128)(2,1)S(1)}, u32[]{:S(2)}, u32[]{:S(2)}) %collective-permute-start.10) | collective-permute-done | bytes 40992 | tf_op jit(solution)/shard_map/ppermute | solution.py:485
  31.2 1.0 %collective-permute-start.11 = (bf16[320,128]{1,0:T(8,128)(2,1)S(1)}, bf16[320,128]{1,0:T(8,128)(2,1)S(1)}, u32[]{:S(2)}, u32[]{:S(2)}) collective-permute-start(bf16[320,128]{1,0:T(8,128)(2,1)S(1)} %shard_map.86.a_ref), channel_id=1, source_target_pairs={{0,8},{1,5},{2,10},{3,7},{4,12},{5,1},{6,14},{7,3},{8,0},{9,13},{1... | collective-permute-start | bytes 245768 | tf_op jit(solution)/shard_map/ppermute | solution.py:485
  32.1 1.9 %collective-permute-done.9.b_ref = bf16[320,128]{1,0:T(8,128)(2,1)S(1)} collective-permute-done((bf16[320,128]{1,0:T(8,128)(2,1)S(1)}, bf16[320,128]{1,0:T(8,128)(2,1)S(1)}, u32[]{:S(2)}, u32[]{:S(2)}) %collective-permute-start.9) | collective-permute-done | bytes 81952 | tf_op jit(solution)/shard_map/ppermute | solution.py:485
  34.0 1.7 %collective-permute-start.12 = (bf16[640,128]{1,0:T(8,128)(2,1)S(1)}, bf16[640,128]{1,0:T(8,128)(2,1)S(1)}, u32[]{:S(2)}, u32[]{:S(2)}) collective-permute-start(bf16[640,128]{1,0:T(8,128)(2,1)S(1)} %shard_map.85.refs_0_), channel_id=1, source_target_pairs={{0,2},{1,9},{2,0},{3,11},{4,6},{5,13},{6,4},{7,15},{8,10},{9,1},{1... | collective-permute-start | bytes 491528 | tf_op jit(solution)/shard_map/ppermute | solution.py:485
  35.7 0.0 collective-permute-done.11.b_ref
  35.8 1.7 %collective-permute-start.13 = (bf16[640,128]{1,0:T(8,128)(2,1)S(1)}, bf16[640,128]{1,0:T(8,128)(2,1)S(1)}, u32[]{:S(2)}, u32[]{:S(2)}) collective-permute-start(bf16[640,128]{1,0:T(8,128)(2,1)S(1)} %shard_map.87.refs_1_), channel_id=1, source_target_pairs={{0,4},{1,3},{2,6},{3,1},{4,0},{5,7},{6,2},{7,5},{8,12},{9,11},{10,... | collective-permute-start | bytes 491528 | tf_op jit(solution)/shard_map/ppermute | solution.py:485
  37.5 0.1 collective-permute-start.14
  37.6 8.1 %collective-permute-done.14.refs_0_ = bf16[560,128]{1,0:T(8,128)(2,1)S(1)} collective-permute-done((bf16[560,128]{1,0:T(8,128)(2,1)S(1)}, bf16[560,128]{1,0:T(8,128)(2,1)S(1)}, u32[]{:S(2)}, u32[]{:S(2)}) %collective-permute-start.14) | collective-permute-done | bytes 143392 | tf_op jit(solution)/shard_map/ppermute | solution.py:503
  45.7 0.0 copy-done.3
  45.7 0.0 copy-done.4
  45.7 2.2 %shard_map.91.short_ref = f32[512,128]{1,0:T(8,128)S(1)} custom-call(f32[3,1024]{1,0:T(4,128)S(1)} %get-tuple-element.60.pos_ref, bf16[1024,128]{1,0:T(8,128)(2,1)S(1)} %get-tuple-element.34.h_ref, bf16[128,128]{1,0:T(8,128)(2,1)S(1)} %bitcast.5, bf16[560,128]{1,0:T(8,128)(2,1)S(1)} %collective-permute-done.14.refs_0_, s32[8,8]{1,0:T(8,128)S(1)} %copy-done.4), custom_call_target="tpu_custom_call" | custom-call | tf_op jit(solution)/shard_map/pallas_call | solution.py:51
  47.9 0.9 %shard_map.88.part_ref = f32[1024,128]{1,0:T(8,128)S(1)} custom-call(bf16[1280,1024]{1,0:T(8,128)(2,1)S(1)} %get-tuple-element.39.p_ref, bf16[640,128]{1,0:T(8,128)(2,1)S(1)} %shard_map.85.refs_0_, bf16[640,128]{1,0:T(8,128)(2,1)S(1)} %shard_map.87.refs_1_), custom_call_target="tpu_custom_call" | custom-call | tf_op jit(solution)/shard_map/pallas_call | solution.py:51
  48.8 0.0 collective-permute-done.12.f_ref
  48.8 0.6 %shard_map.89.part_ref = f32[1024,128]{1,0:T(8,128)S(1)} custom-call(f32[1024,128]{1,0:T(8,128)S(1)} %shard_map.88.part_ref, bf16[640,1024]{1,0:T(8,128)(2,1)S(1)} %get-tuple-element.58.p_ref, bf16[640,128]{1,0:T(8,128)(2,1)S(1)} %collective-permute-done.12.f_ref), custom_call_target="tpu_custom_call" | custom-call | tf_op jit(solution)/shard_map/pallas_call | solution.py:51
  49.4 0.0 collective-permute-done.13.f_ref
  49.4 0.7 %shard_map.92 = (f32[1024,128]{1,0:T(8,128)S(1)}, bf16[1024,128]{1,0:T(8,128)(2,1)S(1)}) custom-call(f32[1024,128]{1,0:T(8,128)S(1)} %shard_map.89.part_ref, bf16[640,1024]{1,0:T(8,128)(2,1)S(1)} %get-tuple-element.59.p_ref, bf16[640,128]{1,0:T(8,128)(2,1)S(1)} %collective-permute-done.13.f_ref, f32[512,128]{1,0:T(8,128)S(1)} %shard_map.91.short_ref), custom_call_target="tpu_custom_call" | custom-call | tf_op jit(solution)/shard_map/pallas_call | solution.py:51
  50.1 0.1 collective-permute-start.15
  50.2 1.5 %collective-permute-done.15.b_ref = bf16[1024,128]{1,0:T(8,128)(2,1)S(1)} collective-permute-done((bf16[1024,128]{1,0:T(8,128)(2,1)S(1)}, bf16[1024,128]{1,0:T(8,128)(2,1)S(1)}, u32[]{:S(2)}, u32[]{:S(2)}) %collective-permute-start.15) | collective-permute-done | bytes 262176 | tf_op jit(solution)/shard_map/ppermute | solution.py:488
  51.7 0.8 %shard_map.93 = bf16[1024,128]{1,0:T(8,128)(2,1)} custom-call(bf16[1024,128]{1,0:T(8,128)(2,1)S(1)} %get-tuple-element.34.h_ref, f32[1024,128]{1,0:T(8,128)S(1)} %get-tuple-element.61.a_ref, bf16[1024,128]{1,0:T(8,128)(2,1)S(1)} %collective-permute-done.15.b_ref), custom_call_target="tpu_custom_call" | custom-call | tf_op jit(solution)/shard_map/pallas_call | solution.py:51
  (10 shorter events, 0.2 us)
Async XLA Ops:
  2.0 6.6 %collective-permute-start.2 = (bf16[640,128]{1,0:T(8,128)(2,1)S(1)}, bf16[640,128]{1,0:T(8,128)(2,1)S(1)}, u32[]{:S(2)}, u32[]{:S(2)}) collective-permute-start(bf16[640,128]{1,0:T(8,128)(2,1)S(1)} %get-tuple-element.46), channel_id=1, source_target_pairs={{0,4},{1,3},{2,6},{3,1},{4,0},{5,7},{6,2},{7,5},{8,12},{9,11},{10,... | collective-permute-start | bytes 491528 | tf_op jit(solution)/shard_map/ppermute | solution.py:485
  5.8 5.4 %collective-permute-start = (bf16[640,128]{1,0:T(8,128)(2,1)S(1)}, bf16[640,128]{1,0:T(8,128)(2,1)S(1)}, u32[]{:S(2)}, u32[]{:S(2)}) collective-permute-start(bf16[640,128]{1,0:T(8,128)(2,1)S(1)} %get-tuple-element.41), channel_id=1, source_target_pairs={{0,2},{1,9},{2,0},{3,11},{4,6},{5,13},{6,4},{7,15},{8,10},{9,1},{1... | collective-permute-start | bytes 491528 | tf_op jit(solution)/shard_map/ppermute | solution.py:485
  7.3 10.0 %copy-start = (f32[1,4096,128]{2,1,0:T(8,128)S(1)}, f32[1,4096,128]{2,1,0:T(8,128)}, u32[]{:S(2)}) copy-start(f32[1,4096,128]{2,1,0:T(8,128)} %param.13) | copy-start | bytes 6291460
  8.6 8.8 %copy-start.1 = (s32[3,4096]{1,0:T(4,128)S(1)}, s32[3,4096]{1,0:T(4,128)}, u32[]{:S(2)}) copy-start(s32[3,4096]{1,0:T(4,128)} %wave_ref.1) | copy-start | bytes 147460
  8.6 4.5 %collective-permute-start.3 = (bf16[320,128]{1,0:T(8,128)(2,1)S(1)}, bf16[320,128]{1,0:T(8,128)(2,1)S(1)}, u32[]{:S(2)}, u32[]{:S(2)}) collective-permute-start(bf16[320,128]{1,0:T(8,128)(2,1)S(1)} %get-tuple-element.48), channel_id=1, source_target_pairs={{0,8},{1,5},{2,10},{3,7},{4,12},{5,1},{6,14},{7,3},{8,0},{9,13},{1... | collective-permute-start | bytes 245768 | tf_op jit(solution)/shard_map/ppermute | solution.py:485
  11.2 4.5 %collective-permute-start.1 = (bf16[320,128]{1,0:T(8,128)(2,1)S(1)}, bf16[320,128]{1,0:T(8,128)(2,1)S(1)}, u32[]{:S(2)}, u32[]{:S(2)}) collective-permute-start(bf16[320,128]{1,0:T(8,128)(2,1)S(1)} %get-tuple-element.43), channel_id=1, source_target_pairs={{0,4},{1,3},{2,6},{3,1},{4,0},{5,7},{6,2},{7,5},{8,12},{9,11},{10,... | collective-permute-start | bytes 245768 | tf_op jit(solution)/shard_map/ppermute | solution.py:485
  13.2 5.2 %collective-permute-start.5 = (bf16[160,128]{1,0:T(8,128)(2,1)S(1)}, bf16[160,128]{1,0:T(8,128)(2,1)S(1)}, u32[]{:S(2)}, u32[]{:S(2)}) collective-permute-start(bf16[160,128]{1,0:T(8,128)(2,1)S(1)} %get-tuple-element.51), channel_id=1, source_target_pairs={{0,2},{1,9},{2,0},{3,11},{4,6},{5,13},{6,4},{7,15},{8,10},{9,1},{1... | collective-permute-start | bytes 122888 | tf_op jit(solution)/shard_map/ppermute | solution.py:485
  15.7 9.5 %copy-start.2 = (f32[1,128,128]{2,1,0:T(8,128)S(1)}, f32[1,128,128]{2,1,0:T(8,128)}, u32[]{:S(2)}) copy-start(f32[1,128,128]{2,1,0:T(8,128)} %param.12) | copy-start | bytes 196612
  15.7 4.1 %collective-permute-start.4 = (bf16[160,128]{1,0:T(8,128)(2,1)S(1)}, bf16[160,128]{1,0:T(8,128)(2,1)S(1)}, u32[]{:S(2)}, u32[]{:S(2)}) collective-permute-start(bf16[160,128]{1,0:T(8,128)(2,1)S(1)} %get-tuple-element.50), channel_id=1, source_target_pairs={{0,8},{1,5},{2,10},{3,7},{4,12},{5,1},{6,14},{7,3},{8,0},{9,13},{1... | collective-permute-start | bytes 122888 | tf_op jit(solution)/shard_map/ppermute | solution.py:485
  18.3 27.4 %copy-start.3 = (bf16[1,128,128]{2,1,0:T(8,128)(2,1)S(1)}, bf16[1,128,128]{2,1,0:T(8,128)(2,1)}, u32[]{:S(2)}) copy-start(bf16[1,128,128]{2,1,0:T(8,128)(2,1)} %param.11) | copy-start | bytes 98308
  18.3 27.4 %copy-start.4 = (s32[8,8]{1,0:T(8,128)S(1)}, s32[8,8]{1,0:T(8,128)}, u32[]{:S(2)}) copy-start(s32[8,8]{1,0:T(8,128)} %refs_1_.1) | copy-start | bytes 772
  18.3 4.2 %collective-permute-start.7 = (f32[160,128]{1,0:T(8,128)S(1)}, f32[160,128]{1,0:T(8,128)S(1)}, u32[]{:S(2)}, u32[]{:S(2)}) collective-permute-start(f32[160,128]{1,0:T(8,128)S(1)} %get-tuple-element.55), channel_id=1, source_target_pairs={{0,1},{1,0},{2,3},{3,2},{4,5},{5,4},{6,7},{7,6},{8,9},{9,8},{10,11... | collective-permute-start | bytes 245768 | tf_op jit(solution)/shard_map/ppermute | solution.py:488
  19.8 5.4 %collective-permute-start.6 = (bf16[320,128]{1,0:T(8,128)(2,1)S(1)}, bf16[320,128]{1,0:T(8,128)(2,1)S(1)}, u32[]{:S(2)}, u32[]{:S(2)}) collective-permute-start(bf16[320,128]{1,0:T(8,128)(2,1)S(1)} %get-tuple-element.53), channel_id=1, source_target_pairs={{0,16},{1,17},{2,18},{3,19},{4,20},{5,21},{6,22},{7,23},{8,24},{9,... | collective-permute-start | bytes 245768 | tf_op jit(solution)/shard_map/ppermute | solution.py:485
  25.5 4.1 %collective-permute-start.8 = (bf16[160,128]{1,0:T(8,128)(2,1)S(1)}, bf16[160,128]{1,0:T(8,128)(2,1)S(1)}, u32[]{:S(2)}, u32[]{:S(2)}) collective-permute-start(bf16[160,128]{1,0:T(8,128)(2,1)S(1)} %get-tuple-element.56.a_ref), channel_id=1, source_target_pairs={{0,8},{1,5},{2,10},{3,7},{4,12},{5,1},{6,14},{7,3},{8,0},{9,13},{1... | collective-permute-start | bytes 122888 | tf_op jit(solution)/shard_map/ppermute | solution.py:485
  27.2 4.0 %collective-permute-start.10 = (bf16[160,128]{1,0:T(8,128)(2,1)S(1)}, bf16[160,128]{1,0:T(8,128)(2,1)S(1)}, u32[]{:S(2)}, u32[]{:S(2)}) collective-permute-start(bf16[160,128]{1,0:T(8,128)(2,1)S(1)} %get-tuple-element.57.a_ref), channel_id=1, source_target_pairs={{0,2},{1,9},{2,0},{3,11},{4,6},{5,13},{6,4},{7,15},{8,10},{9,1},{1... | collective-permute-start | bytes 122888 | tf_op jit(solution)/shard_map/ppermute | solution.py:485
  29.6 4.4 %collective-permute-start.9 = (bf16[320,128]{1,0:T(8,128)(2,1)S(1)}, bf16[320,128]{1,0:T(8,128)(2,1)S(1)}, u32[]{:S(2)}, u32[]{:S(2)}) collective-permute-start(bf16[320,128]{1,0:T(8,128)(2,1)S(1)} %shard_map.84.a_ref), channel_id=1, source_target_pairs={{0,4},{1,3},{2,6},{3,1},{4,0},{5,7},{6,2},{7,5},{8,12},{9,11},{10,... | collective-permute-start | bytes 245768 | tf_op jit(solution)/shard_map/ppermute | solution.py:485
  31.2 4.6 %collective-permute-start.11 = (bf16[320,128]{1,0:T(8,128)(2,1)S(1)}, bf16[320,128]{1,0:T(8,128)(2,1)S(1)}, u32[]{:S(2)}, u32[]{:S(2)}) collective-permute-start(bf16[320,128]{1,0:T(8,128)(2,1)S(1)} %shard_map.86.a_ref), channel_id=1, source_target_pairs={{0,8},{1,5},{2,10},{3,7},{4,12},{5,1},{6,14},{7,3},{8,0},{9,13},{1... | collective-permute-start | bytes 245768 | tf_op jit(solution)/shard_map/ppermute | solution.py:485
  34.0 14.8 %collective-permute-start.12 = (bf16[640,128]{1,0:T(8,128)(2,1)S(1)}, bf16[640,128]{1,0:T(8,128)(2,1)S(1)}, u32[]{:S(2)}, u32[]{:S(2)}) collective-permute-start(bf16[640,128]{1,0:T(8,128)(2,1)S(1)} %shard_map.85.refs_0_), channel_id=1, source_target_pairs={{0,2},{1,9},{2,0},{3,11},{4,6},{5,13},{6,4},{7,15},{8,10},{9,1},{1... | collective-permute-start | bytes 491528 | tf_op jit(solution)/shard_map/ppermute | solution.py:485
  35.8 13.7 %collective-permute-start.13 = (bf16[640,128]{1,0:T(8,128)(2,1)S(1)}, bf16[640,128]{1,0:T(8,128)(2,1)S(1)}, u32[]{:S(2)}, u32[]{:S(2)}) collective-permute-start(bf16[640,128]{1,0:T(8,128)(2,1)S(1)} %shard_map.87.refs_1_), channel_id=1, source_target_pairs={{0,4},{1,3},{2,6},{3,1},{4,0},{5,7},{6,2},{7,5},{8,12},{9,11},{10,... | collective-permute-start | bytes 491528 | tf_op jit(solution)/shard_map/ppermute | solution.py:485
  37.5 8.2 %collective-permute-start.14 = (bf16[560,128]{1,0:T(8,128)(2,1)S(1)}, bf16[560,128]{1,0:T(8,128)(2,1)S(1)}, u32[]{:S(2)}, u32[]{:S(2)}) collective-permute-start(bf16[560,128]{1,0:T(8,128)(2,1)S(1)} %shard_map.90), channel_id=1, source_target_pairs={{0,31},{1,2},{2,1},{3,4},{4,3},{5,6},{6,5},{7,8},{8,7},{9,10},{10,... | collective-permute-start | bytes 430088 | tf_op jit(solution)/shard_map/ppermute | solution.py:503
  50.1 1.6 %collective-permute-start.15 = (bf16[1024,128]{1,0:T(8,128)(2,1)S(1)}, bf16[1024,128]{1,0:T(8,128)(2,1)S(1)}, u32[]{:S(2)}, u32[]{:S(2)}) collective-permute-start(bf16[1024,128]{1,0:T(8,128)(2,1)S(1)} %get-tuple-element.62), channel_id=1, source_target_pairs={{0,1},{1,0},{2,3},{3,2},{4,5},{5,4},{6,7},{7,6},{8,9},{9,8},{10,11... | collective-permute-start | bytes 786440 | tf_op jit(solution)/shard_map/ppermute | solution.py:488

commit v2 on v1

--- a/solution.py
+++ b/solution.py
@@ -74,7 +74,7 @@
         self.rows = self.slice_rows * self.doms
 
     def order(self, wav, chain):
-        turn = (0, 1, 2, 0)[(CHAINS * wav + chain) % 4]
+        turn = (2, 0, 0, 1)[(CHAINS * wav + chain) % 4]
         first = [0, 1, 2]
         return first[turn:] + first[:turn] + list(range(3, self.bits))
 
@@ -281,19 +281,13 @@
     return call(body, out, mine, other)
 
 
-def add_all(mine, others):
-    rows, channels = mine[0].shape
-
-    def body(*refs):
-        keep_ref, send_ref = refs[-2:]
-        for i in range(CHAINS):
-            at = slice(i * rows, (i + 1) * rows)
-            total = refs[i][...] + refs[CHAINS + i][...].astype(F32)
-            keep_ref[at, :] = total
-            send_ref[at, :] = total.astype(BF16)
-
-    out = [VMEM((CHAINS * rows, channels), t) for t in (F32, BF16)]
-    return call(body, out, *mine, *others)
+def add_both(mine, other):
+    def body(a_ref, b_ref, keep_ref, send_ref):
+        total = a_ref[...] + b_ref[...].astype(F32)
+        keep_ref[...] = total
+        send_ref[...] = total.astype(BF16)
+
+    return call(body, [VMEM(mine.shape, t) for t in (F32, BF16)], mine, other)
 
 
 def add_plain(mine, other):
@@ -307,27 +301,24 @@
     return jnp.dot(a, b, precision=lax.Precision.HIGHEST, preferred_element_type=F32)
 
 
-def filtered(mine, other, mixing, weights):
+def filtered(chain, mine, other, mixing, weights):
     rows, channels = mine.shape
-    part = rows // CHAINS
+    half = rows // 2
     groups = rows // (2 * TILE)
 
     def body(mine_ref, other_ref, mix_ref, *refs):
-        weight_refs, out_refs = refs[:-CHAINS], refs[-CHAINS:]
+        *weight_refs, out_ref = refs
         there = other_ref[...].astype(F32)
-        cuts = [there[i * part // 2 : (i + 1) * part // 2] for i in range(2 * CHAINS)]
-        there = jnp.concatenate([cuts[i ^ 1] for i in range(2 * CHAINS)], axis=0)
-        mixed = dot_exact(mine_ref[...] + there, mix_ref[...])
-        factor = weight_refs[0][...]
+        total = mine_ref[...] + jnp.concatenate([there[half:], there[:half]], axis=0)
+        mixed = dot_exact(total, mix_ref[...])
+        at = slice(chain * half, (chain + 1) * half)
+        factor = weight_refs[0][at, :]
         for ref in weight_refs[1:]:
-            factor = factor + ref[...]
+            factor = factor + ref[at, :]
         mixed = mixed.reshape(groups, 2, TILE, channels) * factor.reshape(groups, 1, TILE, channels)
-        mixed = mixed.reshape(rows, channels).astype(BF16)
-        for i, ref in enumerate(out_refs):
-            ref[...] = mixed[i * part : (i + 1) * part]
-
-    out = [VMEM((part, channels), BF16)] * CHAINS
-    return call(body, out, mine, other, mixing, *weights)
+        out_ref[...] = mixed.reshape(rows, channels).astype(BF16)
+
+    return call(body, VMEM(mine.shape, BF16), mine, other, mixing, *weights)
 
 
 def join(low, high):
@@ -519,8 +510,10 @@
         for c in each:
             kept[c], leaving = add_split(kept[c], arrived[c])
             arrived[c] = swap(leaving, c, step)
-    total, leaving = add_all(kept, arrived)
-    filts = list(filtered(total, swap(leaving, 0, bits - 1), spectral_mix[0], sums))
+    for c in each:
+        kept[c], leaving = add_both(kept[c], arrived[c])
+        arrived[c] = swap(leaving, c, bits - 1)
+    filts = [filtered(c, kept[c], arrived[c], spectral_mix[0], sums) for c in each]
     for step in reversed(range(1, bits - 1)):
         for c in each:
             filts[c] = join(filts[c], swap(filts[c], c, step))

time: 52.8 us -> 51.9 us (0.983)
  waiting for transfers between devices: 19.5 us -> 17.5 us
  starting transfers between devices: 22.3 us -> 23.3 us
    ppermute x13 -> x14, waiting for transfers between devices: 9.88 us -> 7.87 us  [swap(): return lax.ppermute(x, ('dom', 'wav'), pairs)]
    ppermute x13 -> x14, starting transfers between devices: 22.1 us -> 23.1 us  [swap(): return lax.ppermute(x, ('dom', 'wav'), pairs)]
    pallas_call x21 -> x23, Pallas kernels: 10.5 us -> 10.6 us  [call(): pl.pallas_call(body, in_specs=specs, out_specs=spec if single else [spec]...]
  transfers between devices with their start and end apart: 16 -> 17, of which waited for: 10 -> 10; matrix products, arithmetic and copies ran while one was open for 0% -> 0% of each run, Pallas kernels for 13% -> 14%
where the time goes in v2:
time: 51.9 us; the launch traced here: 51.6 us
  starting transfers between devices  23.3 us (45%)
  waiting for transfers between devices  17.5 us (34%)
  Pallas kernels  10.6 us (20%)
    ppermute x14, starting transfers between devices, swap(): return lax.ppermute(x, ('dom', 'wav'), pairs)  23.1 us
    pallas_call x23, Pallas kernels, call(): pl.pallas_call(body, in_specs=specs, out_specs=spec if single else [spec]...  10.6 us
    ppermute x1, waiting for transfers between devices, local(): halos = [lax.ppermute(packed, ('dom', 'wav'), chain)]  8.11 us
    ppermute x14, waiting for transfers between devices, swap(): return lax.ppermute(x, ('dom', 'wav'), pairs)  7.87 us
    ppermute x2, waiting for transfers between devices, swap_wav(): return lax.ppermute(x, 'wav', [(w, w ^ mask) for w in range(wavs)])  1.52 us
  transfers between devices with their start and end apart: 17, of which 10 were waited for; matrix products, arithmetic and copies ran while one was open for 0% of the time, Pallas kernels for 14%

profile of v2, /device:TPU:0, one launch (start us, length us, event | category | flops | bytes accessed | tf_op | source)
XLA Modules:
  0.0 51.6 jit_solution(8800420557858557385)
XLA Ops:
  0.0 1.3 %shard_map.73 = (f32[296,1024]{1,0:T(8,128)S(1)}, f32[296,1024]{1,0:T(8,128)S(1)}, f32[72,1024]{1,0:T(8,128)S(1)}, f32[72,1024]{1,0:T(8,128)S(1)}, f32[3,1024]{1,0:T(4,128)S(1)}, /*index=5*/bf16[1024,128]{1,0:T(8,128)(2,1)S(1)}) custom-call(f32[3,1024]{1,0:T(4,128)} %pos_hbm.1, bf16[1024,128]{1,0:T(8,128)(2,1)} %h_hbm.1), custom_call_target="tpu_custom_call" | custom-call | tf_op jit(solution)/shard_map/pallas_call | solution.py:51
  1.3 0.7 %shard_map.75 = (bf16[640,1024]{1,0:T(8,128)(2,1)S(1)}, bf16[640,128]{1,0:T(8,128)(2,1)S(1)}) custom-call(f32[296,1024]{1,0:T(8,128)S(1)} %get-tuple-element.35.xyc, f32[296,1024]{1,0:T(8,128)S(1)} %get-tuple-element.36.xys, f32[72,1024]{1,0:T(8,128)S(1)} %get-tuple-element.37.zc, f32[72,1024]{1,0:T(8,128)S(1)} %get-tuple-element.38.zs, ...), custom_call_target="tpu_custom_call" | custom-call | tf_op jit(solution)/shard_map/pallas_call | solution.py:51
  2.0 3.1 %collective-permute-start = (bf16[640,128]{1,0:T(8,128)(2,1)S(1)}, bf16[640,128]{1,0:T(8,128)(2,1)S(1)}, u32[]{:S(2)}, u32[]{:S(2)}) collective-permute-start(bf16[640,128]{1,0:T(8,128)(2,1)S(1)} %get-tuple-element.41), channel_id=1, source_target_pairs={{0,8},{1,3},{2,10},{3,1},{4,12},{5,7},{6,14},{7,5},{8,0},{9,11},{1... | collective-permute-start | bytes 491528 | tf_op jit(solution)/shard_map/ppermute | solution.py:476
  5.1 0.7 %shard_map.83 = (bf16[640,1024]{1,0:T(8,128)(2,1)S(1)}, bf16[640,128]{1,0:T(8,128)(2,1)S(1)}) custom-call(f32[296,1024]{1,0:T(8,128)S(1)} %get-tuple-element.35.xyc, f32[296,1024]{1,0:T(8,128)S(1)} %get-tuple-element.36.xys, f32[72,1024]{1,0:T(8,128)S(1)} %get-tuple-element.37.zc, f32[72,1024]{1,0:T(8,128)S(1)} %get-tuple-element.38.zs, ...), custom_call_target="tpu_custom_call" | custom-call | tf_op jit(solution)/shard_map/pallas_call | solution.py:51
  5.8 0.0 copy-start.2
  5.8 1.6 %collective-permute-start.7 = (bf16[640,128]{1,0:T(8,128)(2,1)S(1)}, bf16[640,128]{1,0:T(8,128)(2,1)S(1)}, u32[]{:S(2)}, u32[]{:S(2)}) collective-permute-start(bf16[640,128]{1,0:T(8,128)(2,1)S(1)} %get-tuple-element.51), channel_id=1, source_target_pairs={{0,2},{1,5},{2,0},{3,7},{4,6},{5,1},{6,4},{7,3},{8,10},{9,13},{10,... | collective-permute-start | bytes 491528 | tf_op jit(solution)/shard_map/ppermute | solution.py:476
  7.4 0.0 copy-start
  7.4 1.2 %shard_map.74 = (bf16[1280,1024]{1,0:T(8,128)(2,1)S(1)}, f32[640,128]{1,0:T(8,128)S(1)}, f32[640,128]{1,0:T(8,128)S(1)}) custom-call(f32[296,1024]{1,0:T(8,128)S(1)} %get-tuple-element.35.xyc, f32[296,1024]{1,0:T(8,128)S(1)} %get-tuple-element.36.xys, f32[72,1024]{1,0:T(8,128)S(1)} %get-tuple-element.37.zc, f32[72,1024]{1,0:T(8,128)S(1)} %get-tuple-element.38.zs, ...), custom_call_target="tpu_custom_call" | custom-call | tf_op jit(solution)/shard_map/pallas_call | solution.py:51
  8.7 0.0 collective-permute-done.b_ref
  8.7 1.7 %collective-permute-start.1 = (bf16[320,128]{1,0:T(8,128)(2,1)S(1)}, bf16[320,128]{1,0:T(8,128)(2,1)S(1)}, u32[]{:S(2)}, u32[]{:S(2)}) collective-permute-start(bf16[320,128]{1,0:T(8,128)(2,1)S(1)} %get-tuple-element.43), channel_id=1, source_target_pairs={{0,2},{1,5},{2,0},{3,7},{4,6},{5,1},{6,4},{7,3},{8,10},{9,13},{10,... | collective-permute-start | bytes 245768 | tf_op jit(solution)/shard_map/ppermute | solution.py:476
  10.4 0.8 %collective-permute-done.7.b_ref = bf16[640,128]{1,0:T(8,128)(2,1)S(1)} collective-permute-done((bf16[640,128]{1,0:T(8,128)(2,1)S(1)}, bf16[640,128]{1,0:T(8,128)(2,1)S(1)}, u32[]{:S(2)}, u32[]{:S(2)}) %collective-permute-start.7) | collective-permute-done | bytes 163872 | tf_op jit(solution)/shard_map/ppermute | solution.py:476
  11.3 1.6 %collective-permute-start.8 = (bf16[320,128]{1,0:T(8,128)(2,1)S(1)}, bf16[320,128]{1,0:T(8,128)(2,1)S(1)}, u32[]{:S(2)}, u32[]{:S(2)}) collective-permute-start(bf16[320,128]{1,0:T(8,128)(2,1)S(1)} %get-tuple-element.53), channel_id=1, source_target_pairs={{0,4},{1,9},{2,6},{3,11},{4,0},{5,13},{6,2},{7,15},{8,12},{9,1},{1... | collective-permute-start | bytes 245768 | tf_op jit(solution)/shard_map/ppermute | solution.py:476
  12.8 0.0 copy-done.2
  12.8 0.0 copy-done
  12.9 0.0 copy-start.1
  12.9 0.9 %shard_map.79 = (f32[160,128]{1,0:T(8,128)S(1)}, f32[160,128]{1,0:T(8,128)S(1)}) custom-call(s32[3,4096]{1,0:T(4,128)S(1)} %copy-done.2, f32[4096,128]{1,0:T(8,128)S(1)} %bitcast.3), custom_call_target="tpu_custom_call" | custom-call | tf_op jit(solution)/shard_map/pallas_call | solution.py:51
  13.8 0.0 collective-permute-done.1.b_ref
  13.8 1.2 %collective-permute-start.2 = (bf16[160,128]{1,0:T(8,128)(2,1)S(1)}, bf16[160,128]{1,0:T(8,128)(2,1)S(1)}, u32[]{:S(2)}, u32[]{:S(2)}) collective-permute-start(bf16[160,128]{1,0:T(8,128)(2,1)S(1)} %get-tuple-element.45), channel_id=1, source_target_pairs={{0,4},{1,9},{2,6},{3,11},{4,0},{5,13},{6,2},{7,15},{8,12},{9,1},{1... | collective-permute-start | bytes 122888 | tf_op jit(solution)/shard_map/ppermute | solution.py:476
  15.0 0.0 collective-permute-start.4
  15.0 0.8 %collective-permute-done.8.b_ref = bf16[320,128]{1,0:T(8,128)(2,1)S(1)} collective-permute-done((bf16[320,128]{1,0:T(8,128)(2,1)S(1)}, bf16[320,128]{1,0:T(8,128)(2,1)S(1)}, u32[]{:S(2)}, u32[]{:S(2)}) %collective-permute-start.8) | collective-permute-done | bytes 81952 | tf_op jit(solution)/shard_map/ppermute | solution.py:476
  15.8 0.0 copy-start.3
  15.8 0.0 copy-start.4
  15.8 0.9 %collective-permute-start.9 = (bf16[160,128]{1,0:T(8,128)(2,1)S(1)}, bf16[160,128]{1,0:T(8,128)(2,1)S(1)}, u32[]{:S(2)}, u32[]{:S(2)}) collective-permute-start(bf16[160,128]{1,0:T(8,128)(2,1)S(1)} %get-tuple-element.55), channel_id=1, source_target_pairs={{0,8},{1,3},{2,10},{3,1},{4,12},{5,7},{6,14},{7,5},{8,0},{9,11},{1... | collective-permute-start | bytes 122888 | tf_op jit(solution)/shard_map/ppermute | solution.py:476
  16.7 1.2 %collective-permute-done.2.b_ref = bf16[160,128]{1,0:T(8,128)(2,1)S(1)} collective-permute-done((bf16[160,128]{1,0:T(8,128)(2,1)S(1)}, bf16[160,128]{1,0:T(8,128)(2,1)S(1)}, u32[]{:S(2)}, u32[]{:S(2)}) %collective-permute-start.2) | collective-permute-done | bytes 40992 | tf_op jit(solution)/shard_map/ppermute | solution.py:476
  17.9 2.7 %collective-permute-start.3 = (bf16[160,128]{1,0:T(8,128)(2,1)S(1)}, bf16[160,128]{1,0:T(8,128)(2,1)S(1)}, u32[]{:S(2)}, u32[]{:S(2)}) collective-permute-start(bf16[160,128]{1,0:T(8,128)(2,1)S(1)} %get-tuple-element.47), channel_id=1, source_target_pairs={{0,16},{1,17},{2,18},{3,19},{4,20},{5,21},{6,22},{7,23},{8,24},{9,... | collective-permute-start | bytes 122888 | tf_op jit(solution)/shard_map/ppermute | solution.py:476
  20.5 0.0 collective-permute-done.9.b_ref
  20.5 2.4 %collective-permute-start.10 = (bf16[160,128]{1,0:T(8,128)(2,1)S(1)}, bf16[160,128]{1,0:T(8,128)(2,1)S(1)}, u32[]{:S(2)}, u32[]{:S(2)}) collective-permute-start(bf16[160,128]{1,0:T(8,128)(2,1)S(1)} %get-tuple-element.57), channel_id=1, source_target_pairs={{0,16},{1,17},{2,18},{3,19},{4,20},{5,21},{6,22},{7,23},{8,24},{9,... | collective-permute-start | bytes 122888 | tf_op jit(solution)/shard_map/ppermute | solution.py:476
  22.9 0.0 collective-permute-done.4.refs_1_
  22.9 0.0 collective-permute-done.3.other_ref
  22.9 0.0 copy-done.1
  22.9 0.2 shard_map.80.a_ref
  23.2 1.4 %collective-permute-start.5 = (bf16[160,128]{1,0:T(8,128)(2,1)S(1)}, bf16[160,128]{1,0:T(8,128)(2,1)S(1)}, u32[]{:S(2)}, u32[]{:S(2)}) collective-permute-start(bf16[160,128]{1,0:T(8,128)(2,1)S(1)} %shard_map.80.a_ref), channel_id=1, source_target_pairs={{0,4},{1,9},{2,6},{3,11},{4,0},{5,13},{6,2},{7,15},{8,12},{9,1},{1... | collective-permute-start | bytes 122888 | tf_op jit(solution)/shard_map/ppermute | solution.py:476
  24.6 0.9 %collective-permute-done.10.other_ref = bf16[160,128]{1,0:T(8,128)(2,1)S(1)} collective-permute-done((bf16[160,128]{1,0:T(8,128)(2,1)S(1)}, bf16[160,128]{1,0:T(8,128)(2,1)S(1)}, u32[]{:S(2)}, u32[]{:S(2)}) %collective-permute-start.10) | collective-permute-done | bytes 40992 | tf_op jit(solution)/shard_map/ppermute | solution.py:476
  25.5 0.2 shard_map.87.a_ref
  25.7 1.7 %collective-permute-start.11 = (bf16[160,128]{1,0:T(8,128)(2,1)S(1)}, bf16[160,128]{1,0:T(8,128)(2,1)S(1)}, u32[]{:S(2)}, u32[]{:S(2)}) collective-permute-start(bf16[160,128]{1,0:T(8,128)(2,1)S(1)} %shard_map.87.a_ref), channel_id=1, source_target_pairs={{0,8},{1,3},{2,10},{3,1},{4,12},{5,7},{6,14},{7,5},{8,0},{9,11},{1... | collective-permute-start | bytes 122888 | tf_op jit(solution)/shard_map/ppermute | solution.py:476
  27.4 0.2 collective-permute-done.5.b_ref
  27.6 1.5 %collective-permute-start.6 = (bf16[320,128]{1,0:T(8,128)(2,1)S(1)}, bf16[320,128]{1,0:T(8,128)(2,1)S(1)}, u32[]{:S(2)}, u32[]{:S(2)}) collective-permute-start(bf16[320,128]{1,0:T(8,128)(2,1)S(1)} %shard_map.81.a_ref), channel_id=1, source_target_pairs={{0,2},{1,5},{2,0},{3,7},{4,6},{5,1},{6,4},{7,3},{8,10},{9,13},{10,... | collective-permute-start | bytes 245768 | tf_op jit(solution)/shard_map/ppermute | solution.py:476
  29.1 0.9 %collective-permute-done.11.b_ref = bf16[160,128]{1,0:T(8,128)(2,1)S(1)} collective-permute-done((bf16[160,128]{1,0:T(8,128)(2,1)S(1)}, bf16[160,128]{1,0:T(8,128)(2,1)S(1)}, u32[]{:S(2)}, u32[]{:S(2)}) %collective-permute-start.11) | collective-permute-done | bytes 40992 | tf_op jit(solution)/shard_map/ppermute | solution.py:476
  30.0 1.1 %collective-permute-start.12 = (bf16[320,128]{1,0:T(8,128)(2,1)S(1)}, bf16[320,128]{1,0:T(8,128)(2,1)S(1)}, u32[]{:S(2)}, u32[]{:S(2)}) collective-permute-start(bf16[320,128]{1,0:T(8,128)(2,1)S(1)} %shard_map.88.a_ref), channel_id=1, source_target_pairs={{0,4},{1,9},{2,6},{3,11},{4,0},{5,13},{6,2},{7,15},{8,12},{9,1},{1... | collective-permute-start | bytes 245768 | tf_op jit(solution)/shard_map/ppermute | solution.py:476
  31.1 1.9 %collective-permute-done.6.b_ref = bf16[320,128]{1,0:T(8,128)(2,1)S(1)} collective-permute-done((bf16[320,128]{1,0:T(8,128)(2,1)S(1)}, bf16[320,128]{1,0:T(8,128)(2,1)S(1)}, u32[]{:S(2)}, u32[]{:S(2)}) %collective-permute-start.6) | collective-permute-done | bytes 81952 | tf_op jit(solution)/shard_map/ppermute | solution.py:476
  33.0 1.1 %collective-permute-start.13 = (bf16[640,128]{1,0:T(8,128)(2,1)S(1)}, bf16[640,128]{1,0:T(8,128)(2,1)S(1)}, u32[]{:S(2)}, u32[]{:S(2)}) collective-permute-start(bf16[640,128]{1,0:T(8,128)(2,1)S(1)} %shard_map.82.refs_0_), channel_id=1, source_target_pairs={{0,8},{1,3},{2,10},{3,1},{4,12},{5,7},{6,14},{7,5},{8,0},{9,11},{1... | collective-permute-start | bytes 491528 | tf_op jit(solution)/shard_map/ppermute | solution.py:476
  34.1 1.3 %collective-permute-done.12.b_ref = bf16[320,128]{1,0:T(8,128)(2,1)S(1)} collective-permute-done((bf16[320,128]{1,0:T(8,128)(2,1)S(1)}, bf16[320,128]{1,0:T(8,128)(2,1)S(1)}, u32[]{:S(2)}, u32[]{:S(2)}) %collective-permute-start.12) | collective-permute-done | bytes 81952 | tf_op jit(solution)/shard_map/ppermute | solution.py:476
  35.4 1.2 %collective-permute-start.14 = (bf16[640,128]{1,0:T(8,128)(2,1)S(1)}, bf16[640,128]{1,0:T(8,128)(2,1)S(1)}, u32[]{:S(2)}, u32[]{:S(2)}) collective-permute-start(bf16[640,128]{1,0:T(8,128)(2,1)S(1)} %shard_map.89.refs_1_), channel_id=1, source_target_pairs={{0,2},{1,5},{2,0},{3,7},{4,6},{5,1},{6,4},{7,3},{8,10},{9,13},{10,... | collective-permute-start | bytes 491528 | tf_op jit(solution)/shard_map/ppermute | solution.py:476
  36.6 0.1 collective-permute-start.15
  36.7 8.1 %collective-permute-done.15.refs_0_ = bf16[560,128]{1,0:T(8,128)(2,1)S(1)} collective-permute-done((bf16[560,128]{1,0:T(8,128)(2,1)S(1)}, bf16[560,128]{1,0:T(8,128)(2,1)S(1)}, u32[]{:S(2)}, u32[]{:S(2)}) %collective-permute-start.15) | collective-permute-done | bytes 143392 | tf_op jit(solution)/shard_map/ppermute | solution.py:494
  44.8 0.0 copy-done.3
  44.8 0.0 copy-done.4
  44.8 2.2 %shard_map.93.short_ref = f32[512,128]{1,0:T(8,128)S(1)} custom-call(f32[3,1024]{1,0:T(4,128)S(1)} %get-tuple-element.60.pos_ref, bf16[1024,128]{1,0:T(8,128)(2,1)S(1)} %get-tuple-element.34.h_ref, bf16[128,128]{1,0:T(8,128)(2,1)S(1)} %bitcast.6, bf16[560,128]{1,0:T(8,128)(2,1)S(1)} %collective-permute-done.15.refs_0_, s32[8,8]{1,0:T(8,128)S(1)} %copy-done.4), custom_call_target="tpu_custom_call" | custom-call | tf_op jit(solution)/shard_map/pallas_call | solution.py:51
  47.0 0.9 %shard_map.90.part_ref = f32[1024,128]{1,0:T(8,128)S(1)} custom-call(bf16[1280,1024]{1,0:T(8,128)(2,1)S(1)} %get-tuple-element.39.p_ref, bf16[640,128]{1,0:T(8,128)(2,1)S(1)} %shard_map.82.refs_0_, bf16[640,128]{1,0:T(8,128)(2,1)S(1)} %shard_map.89.refs_1_), custom_call_target="tpu_custom_call" | custom-call | tf_op jit(solution)/shard_map/pallas_call | solution.py:51
  47.9 0.0 collective-permute-done.13.f_ref
  48.0 0.6 %shard_map.91.part_ref = f32[1024,128]{1,0:T(8,128)S(1)} custom-call(f32[1024,128]{1,0:T(8,128)S(1)} %shard_map.90.part_ref, bf16[640,1024]{1,0:T(8,128)(2,1)S(1)} %get-tuple-element.58.p_ref, bf16[640,128]{1,0:T(8,128)(2,1)S(1)} %collective-permute-done.13.f_ref), custom_call_target="tpu_custom_call" | custom-call | tf_op jit(solution)/shard_map/pallas_call | solution.py:51
  48.5 0.0 collective-permute-done.14.f_ref
  48.5 0.7 %shard_map.94 = (f32[1024,128]{1,0:T(8,128)S(1)}, bf16[1024,128]{1,0:T(8,128)(2,1)S(1)}) custom-call(f32[1024,128]{1,0:T(8,128)S(1)} %shard_map.91.part_ref, bf16[640,1024]{1,0:T(8,128)(2,1)S(1)} %get-tuple-element.59.p_ref, bf16[640,128]{1,0:T(8,128)(2,1)S(1)} %collective-permute-done.14.f_ref, f32[512,128]{1,0:T(8,128)S(1)} %shard_map.93.short_ref), custom_call_target="tpu_custom_call" | custom-call | tf_op jit(solution)/shard_map/pallas_call | solution.py:51
  49.2 0.1 collective-permute-start.16
  49.3 1.5 %collective-permute-done.16.b_ref = bf16[1024,128]{1,0:T(8,128)(2,1)S(1)} collective-permute-done((bf16[1024,128]{1,0:T(8,128)(2,1)S(1)}, bf16[1024,128]{1,0:T(8,128)(2,1)S(1)}, u32[]{:S(2)}, u32[]{:S(2)}) %collective-permute-start.16) | collective-permute-done | bytes 262176 | tf_op jit(solution)/shard_map/ppermute | solution.py:479
  50.8 0.8 %shard_map.95 = bf16[1024,128]{1,0:T(8,128)(2,1)} custom-call(bf16[1024,128]{1,0:T(8,128)(2,1)S(1)} %get-tuple-element.34.h_ref, f32[1024,128]{1,0:T(8,128)S(1)} %get-tuple-element.61.a_ref, bf16[1024,128]{1,0:T(8,128)(2,1)S(1)} %collective-permute-done.16.b_ref), custom_call_target="tpu_custom_call" | custom-call | tf_op jit(solution)/shard_map/pallas_call | solution.py:51
  (11 shorter events, 0.2 us)
Async XLA Ops:
  2.0 6.7 %collective-permute-start = (bf16[640,128]{1,0:T(8,128)(2,1)S(1)}, bf16[640,128]{1,0:T(8,128)(2,1)S(1)}, u32[]{:S(2)}, u32[]{:S(2)}) collective-permute-start(bf16[640,128]{1,0:T(8,128)(2,1)S(1)} %get-tuple-element.41), channel_id=1, source_target_pairs={{0,8},{1,3},{2,10},{3,1},{4,12},{5,7},{6,14},{7,5},{8,0},{9,11},{1... | collective-permute-start | bytes 491528 | tf_op jit(solution)/shard_map/ppermute | solution.py:476
  5.8 7.0 %copy-start.2 = (s32[3,4096]{1,0:T(4,128)S(1)}, s32[3,4096]{1,0:T(4,128)}, u32[]{:S(2)}) copy-start(s32[3,4096]{1,0:T(4,128)} %wave_ref.1) | copy-start | bytes 147460
  5.8 5.4 %collective-permute-start.7 = (bf16[640,128]{1,0:T(8,128)(2,1)S(1)}, bf16[640,128]{1,0:T(8,128)(2,1)S(1)}, u32[]{:S(2)}, u32[]{:S(2)}) collective-permute-start(bf16[640,128]{1,0:T(8,128)(2,1)S(1)} %get-tuple-element.51), channel_id=1, source_target_pairs={{0,2},{1,5},{2,0},{3,7},{4,6},{5,1},{6,4},{7,3},{8,10},{9,13},{10,... | collective-permute-start | bytes 491528 | tf_op jit(solution)/shard_map/ppermute | solution.py:476
  7.4 5.5 %copy-start = (f32[1,4096,128]{2,1,0:T(8,128)S(1)}, f32[1,4096,128]{2,1,0:T(8,128)}, u32[]{:S(2)}) copy-start(f32[1,4096,128]{2,1,0:T(8,128)} %param.13) | copy-start | bytes 6291460
  8.7 5.0 %collective-permute-start.1 = (bf16[320,128]{1,0:T(8,128)(2,1)S(1)}, bf16[320,128]{1,0:T(8,128)(2,1)S(1)}, u32[]{:S(2)}, u32[]{:S(2)}) collective-permute-start(bf16[320,128]{1,0:T(8,128)(2,1)S(1)} %get-tuple-element.43), channel_id=1, source_target_pairs={{0,2},{1,5},{2,0},{3,7},{4,6},{5,1},{6,4},{7,3},{8,10},{9,13},{10,... | collective-permute-start | bytes 245768 | tf_op jit(solution)/shard_map/ppermute | solution.py:476
  11.3 4.5 %collective-permute-start.8 = (bf16[320,128]{1,0:T(8,128)(2,1)S(1)}, bf16[320,128]{1,0:T(8,128)(2,1)S(1)}, u32[]{:S(2)}, u32[]{:S(2)}) collective-permute-start(bf16[320,128]{1,0:T(8,128)(2,1)S(1)} %get-tuple-element.53), channel_id=1, source_target_pairs={{0,4},{1,9},{2,6},{3,11},{4,0},{5,13},{6,2},{7,15},{8,12},{9,1},{1... | collective-permute-start | bytes 245768 | tf_op jit(solution)/shard_map/ppermute | solution.py:476
  12.9 10.1 %copy-start.1 = (f32[1,128,128]{2,1,0:T(8,128)S(1)}, f32[1,128,128]{2,1,0:T(8,128)}, u32[]{:S(2)}) copy-start(f32[1,128,128]{2,1,0:T(8,128)} %param.12) | copy-start | bytes 196612
  13.8 4.1 %collective-permute-start.2 = (bf16[160,128]{1,0:T(8,128)(2,1)S(1)}, bf16[160,128]{1,0:T(8,128)(2,1)S(1)}, u32[]{:S(2)}, u32[]{:S(2)}) collective-permute-start(bf16[160,128]{1,0:T(8,128)(2,1)S(1)} %get-tuple-element.45), channel_id=1, source_target_pairs={{0,4},{1,9},{2,6},{3,11},{4,0},{5,13},{6,2},{7,15},{8,12},{9,1},{1... | collective-permute-start | bytes 122888 | tf_op jit(solution)/shard_map/ppermute | solution.py:476
  15.0 7.9 %collective-permute-start.4 = (f32[160,128]{1,0:T(8,128)S(1)}, f32[160,128]{1,0:T(8,128)S(1)}, u32[]{:S(2)}, u32[]{:S(2)}) collective-permute-start(f32[160,128]{1,0:T(8,128)S(1)} %get-tuple-element.49), channel_id=1, source_target_pairs={{0,1},{1,0},{2,3},{3,2},{4,5},{5,4},{6,7},{7,6},{8,9},{9,8},{10,11... | collective-permute-start | bytes 245768 | tf_op jit(solution)/shard_map/ppermute | solution.py:479
  15.8 29.0 %copy-start.3 = (bf16[1,128,128]{2,1,0:T(8,128)(2,1)S(1)}, bf16[1,128,128]{2,1,0:T(8,128)(2,1)}, u32[]{:S(2)}) copy-start(bf16[1,128,128]{2,1,0:T(8,128)(2,1)} %param.11) | copy-start | bytes 98308
  15.8 29.0 %copy-start.4 = (s32[8,8]{1,0:T(8,128)S(1)}, s32[8,8]{1,0:T(8,128)}, u32[]{:S(2)}) copy-start(s32[8,8]{1,0:T(8,128)} %refs_1_.1) | copy-start | bytes 772
  15.8 4.7 %collective-permute-start.9 = (bf16[160,128]{1,0:T(8,128)(2,1)S(1)}, bf16[160,128]{1,0:T(8,128)(2,1)S(1)}, u32[]{:S(2)}, u32[]{:S(2)}) collective-permute-start(bf16[160,128]{1,0:T(8,128)(2,1)S(1)} %get-tuple-element.55), channel_id=1, source_target_pairs={{0,8},{1,3},{2,10},{3,1},{4,12},{5,7},{6,14},{7,5},{8,0},{9,11},{1... | collective-permute-start | bytes 122888 | tf_op jit(solution)/shard_map/ppermute | solution.py:476
  17.9 5.1 %collective-permute-start.3 = (bf16[160,128]{1,0:T(8,128)(2,1)S(1)}, bf16[160,128]{1,0:T(8,128)(2,1)S(1)}, u32[]{:S(2)}, u32[]{:S(2)}) collective-permute-start(bf16[160,128]{1,0:T(8,128)(2,1)S(1)} %get-tuple-element.47), channel_id=1, source_target_pairs={{0,16},{1,17},{2,18},{3,19},{4,20},{5,21},{6,22},{7,23},{8,24},{9,... | collective-permute-start | bytes 122888 | tf_op jit(solution)/shard_map/ppermute | solution.py:476
  20.5 5.0 %collective-permute-start.10 = (bf16[160,128]{1,0:T(8,128)(2,1)S(1)}, bf16[160,128]{1,0:T(8,128)(2,1)S(1)}, u32[]{:S(2)}, u32[]{:S(2)}) collective-permute-start(bf16[160,128]{1,0:T(8,128)(2,1)S(1)} %get-tuple-element.57), channel_id=1, source_target_pairs={{0,16},{1,17},{2,18},{3,19},{4,20},{5,21},{6,22},{7,23},{8,24},{9,... | collective-permute-start | bytes 122888 | tf_op jit(solution)/shard_map/ppermute | solution.py:476
  23.2 4.5 %collective-permute-start.5 = (bf16[160,128]{1,0:T(8,128)(2,1)S(1)}, bf16[160,128]{1,0:T(8,128)(2,1)S(1)}, u32[]{:S(2)}, u32[]{:S(2)}) collective-permute-start(bf16[160,128]{1,0:T(8,128)(2,1)S(1)} %shard_map.80.a_ref), channel_id=1, source_target_pairs={{0,4},{1,9},{2,6},{3,11},{4,0},{5,13},{6,2},{7,15},{8,12},{9,1},{1... | collective-permute-start | bytes 122888 | tf_op jit(solution)/shard_map/ppermute | solution.py:476
  25.7 4.3 %collective-permute-start.11 = (bf16[160,128]{1,0:T(8,128)(2,1)S(1)}, bf16[160,128]{1,0:T(8,128)(2,1)S(1)}, u32[]{:S(2)}, u32[]{:S(2)}) collective-permute-start(bf16[160,128]{1,0:T(8,128)(2,1)S(1)} %shard_map.87.a_ref), channel_id=1, source_target_pairs={{0,8},{1,3},{2,10},{3,1},{4,12},{5,7},{6,14},{7,5},{8,0},{9,11},{1... | collective-permute-start | bytes 122888 | tf_op jit(solution)/shard_map/ppermute | solution.py:476
  27.6 5.3 %collective-permute-start.6 = (bf16[320,128]{1,0:T(8,128)(2,1)S(1)}, bf16[320,128]{1,0:T(8,128)(2,1)S(1)}, u32[]{:S(2)}, u32[]{:S(2)}) collective-permute-start(bf16[320,128]{1,0:T(8,128)(2,1)S(1)} %shard_map.81.a_ref), channel_id=1, source_target_pairs={{0,2},{1,5},{2,0},{3,7},{4,6},{5,1},{6,4},{7,3},{8,10},{9,13},{10,... | collective-permute-start | bytes 245768 | tf_op jit(solution)/shard_map/ppermute | solution.py:476
  30.0 5.3 %collective-permute-start.12 = (bf16[320,128]{1,0:T(8,128)(2,1)S(1)}, bf16[320,128]{1,0:T(8,128)(2,1)S(1)}, u32[]{:S(2)}, u32[]{:S(2)}) collective-permute-start(bf16[320,128]{1,0:T(8,128)(2,1)S(1)} %shard_map.88.a_ref), channel_id=1, source_target_pairs={{0,4},{1,9},{2,6},{3,11},{4,0},{5,13},{6,2},{7,15},{8,12},{9,1},{1... | collective-permute-start | bytes 245768 | tf_op jit(solution)/shard_map/ppermute | solution.py:476
  33.0 15.0 %collective-permute-start.13 = (bf16[640,128]{1,0:T(8,128)(2,1)S(1)}, bf16[640,128]{1,0:T(8,128)(2,1)S(1)}, u32[]{:S(2)}, u32[]{:S(2)}) collective-permute-start(bf16[640,128]{1,0:T(8,128)(2,1)S(1)} %shard_map.82.refs_0_), channel_id=1, source_target_pairs={{0,8},{1,3},{2,10},{3,1},{4,12},{5,7},{6,14},{7,5},{8,0},{9,11},{1... | collective-permute-start | bytes 491528 | tf_op jit(solution)/shard_map/ppermute | solution.py:476
  35.4 13.1 %collective-permute-start.14 = (bf16[640,128]{1,0:T(8,128)(2,1)S(1)}, bf16[640,128]{1,0:T(8,128)(2,1)S(1)}, u32[]{:S(2)}, u32[]{:S(2)}) collective-permute-start(bf16[640,128]{1,0:T(8,128)(2,1)S(1)} %shard_map.89.refs_1_), channel_id=1, source_target_pairs={{0,2},{1,5},{2,0},{3,7},{4,6},{5,1},{6,4},{7,3},{8,10},{9,13},{10,... | collective-permute-start | bytes 491528 | tf_op jit(solution)/shard_map/ppermute | solution.py:476
  36.6 8.2 %collective-permute-start.15 = (bf16[560,128]{1,0:T(8,128)(2,1)S(1)}, bf16[560,128]{1,0:T(8,128)(2,1)S(1)}, u32[]{:S(2)}, u32[]{:S(2)}) collective-permute-start(bf16[560,128]{1,0:T(8,128)(2,1)S(1)} %shard_map.92), channel_id=1, source_target_pairs={{0,31},{1,2},{2,1},{3,4},{4,3},{5,6},{6,5},{7,8},{8,7},{9,10},{10,... | collective-permute-start | bytes 430088 | tf_op jit(solution)/shard_map/ppermute | solution.py:494
  49.2 1.6 %collective-permute-start.16 = (bf16[1024,128]{1,0:T(8,128)(2,1)S(1)}, bf16[1024,128]{1,0:T(8,128)(2,1)S(1)}, u32[]{:S(2)}, u32[]{:S(2)}) collective-permute-start(bf16[1024,128]{1,0:T(8,128)(2,1)S(1)} %get-tuple-element.62), channel_id=1, source_target_pairs={{0,1},{1,0},{2,3},{3,2},{4,5},{5,4},{6,7},{7,6},{8,9},{9,8},{10,11... | collective-permute-start | bytes 786440 | tf_op jit(solution)/shard_map/ppermute | solution.py:479

commit v3 on v2

--- a/solution.py
+++ b/solution.py
@@ -23,6 +23,7 @@
 
 TILE = 8
 CHAINS = 2
+TURNS = (((2, 1, 0), (0, 1, 2)), ((0, 1, 2), (1, 2, 0)))
 Q_TILES = 2 * SPAN + 3
 Q_ROWS = Q_TILES * TILE
 FIRST_TILE = 2 + 2 * TOP
@@ -74,9 +75,7 @@
         self.rows = self.slice_rows * self.doms
 
     def order(self, wav, chain):
-        turn = (2, 0, 0, 1)[(CHAINS * wav + chain) % 4]
-        first = [0, 1, 2]
-        return first[turn:] + first[:turn] + list(range(3, self.bits))
+        return [*TURNS[wav % 2][chain], *range(3, self.bits)]
 
     def code(self, wav, chain):
         dom = lax.axis_index("dom")

time: 51.9 us -> 52.3 us (level)
  waiting for transfers between devices: 17.5 us -> 20.2 us
  starting transfers between devices: 23.3 us -> 21 us
    ppermute x14, waiting for transfers between devices: 7.87 us -> 10.6 us  [swap(): return lax.ppermute(x, ('dom', 'wav'), pairs)]
    ppermute x14, starting transfers between devices: 23.1 us -> 20.8 us  [swap(): return lax.ppermute(x, ('dom', 'wav'), pairs)]
where the time goes in v3:
time: 52.3 us; the launch traced here: 52 us
  starting transfers between devices  21 us (40%)
  waiting for transfers between devices  20.2 us (39%)
  Pallas kernels  10.7 us (20%)
    ppermute x14, starting transfers between devices, swap(): return lax.ppermute(x, ('dom', 'wav'), pairs)  20.8 us
    pallas_call x23, Pallas kernels, call(): pl.pallas_call(body, in_specs=specs, out_specs=spec if single else [spec]...  10.7 us
    ppermute x14, waiting for transfers between devices, swap(): return lax.ppermute(x, ('dom', 'wav'), pairs)  10.6 us
    ppermute x1, waiting for transfers between devices, local(): halos = [lax.ppermute(packed, ('dom', 'wav'), chain)]  8.11 us
    ppermute x2, waiting for transfers between devices, swap_wav(): return lax.ppermute(x, 'wav', [(w, w ^ mask) for w in range(wavs)])  1.52 us
  transfers between devices with their start and end apart: 17, of which 10 were waited for; matrix products, arithmetic and copies ran while one was open for 0% of the time, Pallas kernels for 14%

profile of v3, /device:TPU:0, one launch (start us, length us, event | category | flops | bytes accessed | tf_op | source)
XLA Modules:
  0.0 52.0 jit_solution(8981548493551944665)
XLA Ops:
  0.0 1.3 %shard_map.73 = (f32[296,1024]{1,0:T(8,128)S(1)}, f32[296,1024]{1,0:T(8,128)S(1)}, f32[72,1024]{1,0:T(8,128)S(1)}, f32[72,1024]{1,0:T(8,128)S(1)}, f32[3,1024]{1,0:T(4,128)S(1)}, /*index=5*/bf16[1024,128]{1,0:T(8,128)(2,1)S(1)}) custom-call(f32[3,1024]{1,0:T(4,128)} %pos_hbm.1, bf16[1024,128]{1,0:T(8,128)(2,1)} %h_hbm.1), custom_call_target="tpu_custom_call" | custom-call | tf_op jit(solution)/shard_map/pallas_call | solution.py:52
  1.3 0.7 %shard_map.75 = (bf16[640,1024]{1,0:T(8,128)(2,1)S(1)}, bf16[640,128]{1,0:T(8,128)(2,1)S(1)}) custom-call(f32[296,1024]{1,0:T(8,128)S(1)} %get-tuple-element.35.xyc, f32[296,1024]{1,0:T(8,128)S(1)} %get-tuple-element.36.xys, f32[72,1024]{1,0:T(8,128)S(1)} %get-tuple-element.37.zc, f32[72,1024]{1,0:T(8,128)S(1)} %get-tuple-element.38.zs, ...), custom_call_target="tpu_custom_call" | custom-call | tf_op jit(solution)/shard_map/pallas_call | solution.py:52
  2.0 3.1 %collective-permute-start = (bf16[640,128]{1,0:T(8,128)(2,1)S(1)}, bf16[640,128]{1,0:T(8,128)(2,1)S(1)}, u32[]{:S(2)}, u32[]{:S(2)}) collective-permute-start(bf16[640,128]{1,0:T(8,128)(2,1)S(1)} %get-tuple-element.41), channel_id=1, source_target_pairs={{0,8},{1,3},{2,10},{3,1},{4,12},{5,7},{6,14},{7,5},{8,0},{9,11},{1... | collective-permute-start | bytes 491528 | tf_op jit(solution)/shard_map/ppermute | solution.py:475
  5.1 0.7 %shard_map.83 = (bf16[640,1024]{1,0:T(8,128)(2,1)S(1)}, bf16[640,128]{1,0:T(8,128)(2,1)S(1)}) custom-call(f32[296,1024]{1,0:T(8,128)S(1)} %get-tuple-element.35.xyc, f32[296,1024]{1,0:T(8,128)S(1)} %get-tuple-element.36.xys, f32[72,1024]{1,0:T(8,128)S(1)} %get-tuple-element.37.zc, f32[72,1024]{1,0:T(8,128)S(1)} %get-tuple-element.38.zs, ...), custom_call_target="tpu_custom_call" | custom-call | tf_op jit(solution)/shard_map/pallas_call | solution.py:52
  5.8 0.0 copy-start.2
  5.8 1.6 %collective-permute-start.7 = (bf16[640,128]{1,0:T(8,128)(2,1)S(1)}, bf16[640,128]{1,0:T(8,128)(2,1)S(1)}, u32[]{:S(2)}, u32[]{:S(2)}) collective-permute-start(bf16[640,128]{1,0:T(8,128)(2,1)S(1)} %get-tuple-element.51), channel_id=1, source_target_pairs={{0,2},{1,5},{2,0},{3,7},{4,6},{5,1},{6,4},{7,3},{8,10},{9,13},{10,... | collective-permute-start | bytes 491528 | tf_op jit(solution)/shard_map/ppermute | solution.py:475
  7.4 0.0 copy-start
  7.4 1.2 %shard_map.74 = (bf16[1280,1024]{1,0:T(8,128)(2,1)S(1)}, f32[640,128]{1,0:T(8,128)S(1)}, f32[640,128]{1,0:T(8,128)S(1)}) custom-call(f32[296,1024]{1,0:T(8,128)S(1)} %get-tuple-element.35.xyc, f32[296,1024]{1,0:T(8,128)S(1)} %get-tuple-element.36.xys, f32[72,1024]{1,0:T(8,128)S(1)} %get-tuple-element.37.zc, f32[72,1024]{1,0:T(8,128)S(1)} %get-tuple-element.38.zs, ...), custom_call_target="tpu_custom_call" | custom-call | tf_op jit(solution)/shard_map/pallas_call | solution.py:52
  8.7 0.0 collective-permute-done.b_ref
  8.7 1.8 %collective-permute-start.1 = (bf16[320,128]{1,0:T(8,128)(2,1)S(1)}, bf16[320,128]{1,0:T(8,128)(2,1)S(1)}, u32[]{:S(2)}, u32[]{:S(2)}) collective-permute-start(bf16[320,128]{1,0:T(8,128)(2,1)S(1)} %get-tuple-element.43), channel_id=1, source_target_pairs={{0,4},{1,5},{2,6},{3,7},{4,0},{5,1},{6,2},{7,3},{8,12},{9,13},{10,... | collective-permute-start | bytes 245768 | tf_op jit(solution)/shard_map/ppermute | solution.py:475
  10.5 0.7 %collective-permute-done.7.b_ref = bf16[640,128]{1,0:T(8,128)(2,1)S(1)} collective-permute-done((bf16[640,128]{1,0:T(8,128)(2,1)S(1)}, bf16[640,128]{1,0:T(8,128)(2,1)S(1)}, u32[]{:S(2)}, u32[]{:S(2)}) %collective-permute-start.7) | collective-permute-done | bytes 163872 | tf_op jit(solution)/shard_map/ppermute | solution.py:475
  11.3 1.6 %collective-permute-start.8 = (bf16[320,128]{1,0:T(8,128)(2,1)S(1)}, bf16[320,128]{1,0:T(8,128)(2,1)S(1)}, u32[]{:S(2)}, u32[]{:S(2)}) collective-permute-start(bf16[320,128]{1,0:T(8,128)(2,1)S(1)} %get-tuple-element.53), channel_id=1, source_target_pairs={{0,4},{1,9},{2,6},{3,11},{4,0},{5,13},{6,2},{7,15},{8,12},{9,1},{1... | collective-permute-start | bytes 245768 | tf_op jit(solution)/shard_map/ppermute | solution.py:475
  12.8 0.0 copy-done.2
  12.8 0.0 copy-done
  12.9 0.0 copy-start.1
  12.9 0.9 %shard_map.79 = (f32[160,128]{1,0:T(8,128)S(1)}, f32[160,128]{1,0:T(8,128)S(1)}) custom-call(s32[3,4096]{1,0:T(4,128)S(1)} %copy-done.2, f32[4096,128]{1,0:T(8,128)S(1)} %bitcast.3), custom_call_target="tpu_custom_call" | custom-call | tf_op jit(solution)/shard_map/pallas_call | solution.py:52
  13.8 0.0 collective-permute-done.1.b_ref
  13.8 1.6 %collective-permute-start.2 = (bf16[160,128]{1,0:T(8,128)(2,1)S(1)}, bf16[160,128]{1,0:T(8,128)(2,1)S(1)}, u32[]{:S(2)}, u32[]{:S(2)}) collective-permute-start(bf16[160,128]{1,0:T(8,128)(2,1)S(1)} %get-tuple-element.45), channel_id=1, source_target_pairs={{0,2},{1,9},{2,0},{3,11},{4,6},{5,13},{6,4},{7,15},{8,10},{9,1},{1... | collective-permute-start | bytes 122888 | tf_op jit(solution)/shard_map/ppermute | solution.py:475
  15.3 0.0 collective-permute-start.4
  15.3 0.4 collective-permute-done.8.b_ref
  15.8 0.0 copy-start.3
  15.8 0.0 copy-start.4
  15.8 0.9 %collective-permute-start.9 = (bf16[160,128]{1,0:T(8,128)(2,1)S(1)}, bf16[160,128]{1,0:T(8,128)(2,1)S(1)}, u32[]{:S(2)}, u32[]{:S(2)}) collective-permute-start(bf16[160,128]{1,0:T(8,128)(2,1)S(1)} %get-tuple-element.55), channel_id=1, source_target_pairs={{0,8},{1,3},{2,10},{3,1},{4,12},{5,7},{6,14},{7,5},{8,0},{9,11},{1... | collective-permute-start | bytes 122888 | tf_op jit(solution)/shard_map/ppermute | solution.py:475
  16.7 1.2 %collective-permute-done.2.b_ref = bf16[160,128]{1,0:T(8,128)(2,1)S(1)} collective-permute-done((bf16[160,128]{1,0:T(8,128)(2,1)S(1)}, bf16[160,128]{1,0:T(8,128)(2,1)S(1)}, u32[]{:S(2)}, u32[]{:S(2)}) %collective-permute-start.2) | collective-permute-done | bytes 40992 | tf_op jit(solution)/shard_map/ppermute | solution.py:475
  17.9 2.7 %collective-permute-start.3 = (bf16[160,128]{1,0:T(8,128)(2,1)S(1)}, bf16[160,128]{1,0:T(8,128)(2,1)S(1)}, u32[]{:S(2)}, u32[]{:S(2)}) collective-permute-start(bf16[160,128]{1,0:T(8,128)(2,1)S(1)} %get-tuple-element.47), channel_id=1, source_target_pairs={{0,16},{1,17},{2,18},{3,19},{4,20},{5,21},{6,22},{7,23},{8,24},{9,... | collective-permute-start | bytes 122888 | tf_op jit(solution)/shard_map/ppermute | solution.py:475
  20.5 0.0 collective-permute-done.9.b_ref
  20.5 2.0 %collective-permute-start.10 = (bf16[160,128]{1,0:T(8,128)(2,1)S(1)}, bf16[160,128]{1,0:T(8,128)(2,1)S(1)}, u32[]{:S(2)}, u32[]{:S(2)}) collective-permute-start(bf16[160,128]{1,0:T(8,128)(2,1)S(1)} %get-tuple-element.57), channel_id=1, source_target_pairs={{0,16},{1,17},{2,18},{3,19},{4,20},{5,21},{6,22},{7,23},{8,24},{9,... | collective-permute-start | bytes 122888 | tf_op jit(solution)/shard_map/ppermute | solution.py:475
  22.5 0.0 collective-permute-done.4.refs_1_
  22.5 1.6 %collective-permute-done.3.other_ref = bf16[160,128]{1,0:T(8,128)(2,1)S(1)} collective-permute-done((bf16[160,128]{1,0:T(8,128)(2,1)S(1)}, bf16[160,128]{1,0:T(8,128)(2,1)S(1)}, u32[]{:S(2)}, u32[]{:S(2)}) %collective-permute-start.3) | collective-permute-done | bytes 40992 | tf_op jit(solution)/shard_map/ppermute | solution.py:475
  24.1 0.0 copy-done.1
  24.1 0.2 shard_map.80.a_ref
  24.4 1.5 %collective-permute-start.5 = (bf16[160,128]{1,0:T(8,128)(2,1)S(1)}, bf16[160,128]{1,0:T(8,128)(2,1)S(1)}, u32[]{:S(2)}, u32[]{:S(2)}) collective-permute-start(bf16[160,128]{1,0:T(8,128)(2,1)S(1)} %shard_map.80.a_ref), channel_id=1, source_target_pairs={{0,2},{1,9},{2,0},{3,11},{4,6},{5,13},{6,4},{7,15},{8,10},{9,1},{1... | collective-permute-start | bytes 122888 | tf_op jit(solution)/shard_map/ppermute | solution.py:475
  25.9 0.0 collective-permute-done.10.other_ref
  25.9 0.2 shard_map.87.a_ref
  26.1 0.9 %collective-permute-start.11 = (bf16[160,128]{1,0:T(8,128)(2,1)S(1)}, bf16[160,128]{1,0:T(8,128)(2,1)S(1)}, u32[]{:S(2)}, u32[]{:S(2)}) collective-permute-start(bf16[160,128]{1,0:T(8,128)(2,1)S(1)} %shard_map.87.a_ref), channel_id=1, source_target_pairs={{0,8},{1,3},{2,10},{3,1},{4,12},{5,7},{6,14},{7,5},{8,0},{9,11},{1... | collective-permute-start | bytes 122888 | tf_op jit(solution)/shard_map/ppermute | solution.py:475
  27.0 1.4 %collective-permute-done.5.b_ref = bf16[160,128]{1,0:T(8,128)(2,1)S(1)} collective-permute-done((bf16[160,128]{1,0:T(8,128)(2,1)S(1)}, bf16[160,128]{1,0:T(8,128)(2,1)S(1)}, u32[]{:S(2)}, u32[]{:S(2)}) %collective-permute-start.5) | collective-permute-done | bytes 40992 | tf_op jit(solution)/shard_map/ppermute | solution.py:475
  28.4 0.3 collective-permute-start.6
  28.7 1.6 %collective-permute-done.11.b_ref = bf16[160,128]{1,0:T(8,128)(2,1)S(1)} collective-permute-done((bf16[160,128]{1,0:T(8,128)(2,1)S(1)}, bf16[160,128]{1,0:T(8,128)(2,1)S(1)}, u32[]{:S(2)}, u32[]{:S(2)}) %collective-permute-start.11) | collective-permute-done | bytes 40992 | tf_op jit(solution)/shard_map/ppermute | solution.py:475
  30.3 1.2 %collective-permute-start.12 = (bf16[320,128]{1,0:T(8,128)(2,1)S(1)}, bf16[320,128]{1,0:T(8,128)(2,1)S(1)}, u32[]{:S(2)}, u32[]{:S(2)}) collective-permute-start(bf16[320,128]{1,0:T(8,128)(2,1)S(1)} %shard_map.88.a_ref), channel_id=1, source_target_pairs={{0,4},{1,9},{2,6},{3,11},{4,0},{5,13},{6,2},{7,15},{8,12},{9,1},{1... | collective-permute-start | bytes 245768 | tf_op jit(solution)/shard_map/ppermute | solution.py:475
  31.5 1.3 %collective-permute-done.6.b_ref = bf16[320,128]{1,0:T(8,128)(2,1)S(1)} collective-permute-done((bf16[320,128]{1,0:T(8,128)(2,1)S(1)}, bf16[320,128]{1,0:T(8,128)(2,1)S(1)}, u32[]{:S(2)}, u32[]{:S(2)}) %collective-permute-start.6) | collective-permute-done | bytes 81952 | tf_op jit(solution)/shard_map/ppermute | solution.py:475
  32.9 0.5 collective-permute-start.13
  33.4 2.3 %collective-permute-done.12.b_ref = bf16[320,128]{1,0:T(8,128)(2,1)S(1)} collective-permute-done((bf16[320,128]{1,0:T(8,128)(2,1)S(1)}, bf16[320,128]{1,0:T(8,128)(2,1)S(1)}, u32[]{:S(2)}, u32[]{:S(2)}) %collective-permute-start.12) | collective-permute-done | bytes 81952 | tf_op jit(solution)/shard_map/ppermute | solution.py:475
  35.7 1.3 %collective-permute-start.14 = (bf16[640,128]{1,0:T(8,128)(2,1)S(1)}, bf16[640,128]{1,0:T(8,128)(2,1)S(1)}, u32[]{:S(2)}, u32[]{:S(2)}) collective-permute-start(bf16[640,128]{1,0:T(8,128)(2,1)S(1)} %shard_map.89.refs_1_), channel_id=1, source_target_pairs={{0,2},{1,5},{2,0},{3,7},{4,6},{5,1},{6,4},{7,3},{8,10},{9,13},{10,... | collective-permute-start | bytes 491528 | tf_op jit(solution)/shard_map/ppermute | solution.py:475
  37.0 0.1 collective-permute-start.15
  37.1 8.1 %collective-permute-done.15.refs_0_ = bf16[560,128]{1,0:T(8,128)(2,1)S(1)} collective-permute-done((bf16[560,128]{1,0:T(8,128)(2,1)S(1)}, bf16[560,128]{1,0:T(8,128)(2,1)S(1)}, u32[]{:S(2)}, u32[]{:S(2)}) %collective-permute-start.15) | collective-permute-done | bytes 143392 | tf_op jit(solution)/shard_map/ppermute | solution.py:493
  45.2 0.0 copy-done.3
  45.2 0.0 copy-done.4
  45.2 2.2 %shard_map.93.short_ref = f32[512,128]{1,0:T(8,128)S(1)} custom-call(f32[3,1024]{1,0:T(4,128)S(1)} %get-tuple-element.60.pos_ref, bf16[1024,128]{1,0:T(8,128)(2,1)S(1)} %get-tuple-element.34.h_ref, bf16[128,128]{1,0:T(8,128)(2,1)S(1)} %bitcast.6, bf16[560,128]{1,0:T(8,128)(2,1)S(1)} %collective-permute-done.15.refs_0_, s32[8,8]{1,0:T(8,128)S(1)} %copy-done.4), custom_call_target="tpu_custom_call" | custom-call | tf_op jit(solution)/shard_map/pallas_call | solution.py:52
  47.4 0.9 %shard_map.90.part_ref = f32[1024,128]{1,0:T(8,128)S(1)} custom-call(bf16[1280,1024]{1,0:T(8,128)(2,1)S(1)} %get-tuple-element.39.p_ref, bf16[640,128]{1,0:T(8,128)(2,1)S(1)} %shard_map.82.refs_0_, bf16[640,128]{1,0:T(8,128)(2,1)S(1)} %shard_map.89.refs_1_), custom_call_target="tpu_custom_call" | custom-call | tf_op jit(solution)/shard_map/pallas_call | solution.py:52
  48.4 0.0 collective-permute-done.13.f_ref
  48.4 0.6 %shard_map.91.part_ref = f32[1024,128]{1,0:T(8,128)S(1)} custom-call(f32[1024,128]{1,0:T(8,128)S(1)} %shard_map.90.part_ref, bf16[640,1024]{1,0:T(8,128)(2,1)S(1)} %get-tuple-element.58.p_ref, bf16[640,128]{1,0:T(8,128)(2,1)S(1)} %collective-permute-done.13.f_ref), custom_call_target="tpu_custom_call" | custom-call | tf_op jit(solution)/shard_map/pallas_call | solution.py:52
  48.9 0.0 collective-permute-done.14.f_ref
  48.9 0.7 %shard_map.94 = (f32[1024,128]{1,0:T(8,128)S(1)}, bf16[1024,128]{1,0:T(8,128)(2,1)S(1)}) custom-call(f32[1024,128]{1,0:T(8,128)S(1)} %shard_map.91.part_ref, bf16[640,1024]{1,0:T(8,128)(2,1)S(1)} %get-tuple-element.59.p_ref, bf16[640,128]{1,0:T(8,128)(2,1)S(1)} %collective-permute-done.14.f_ref, f32[512,128]{1,0:T(8,128)S(1)} %shard_map.93.short_ref), custom_call_target="tpu_custom_call" | custom-call | tf_op jit(solution)/shard_map/pallas_call | solution.py:52
  49.6 0.1 collective-permute-start.16
  49.7 1.5 %collective-permute-done.16.b_ref = bf16[1024,128]{1,0:T(8,128)(2,1)S(1)} collective-permute-done((bf16[1024,128]{1,0:T(8,128)(2,1)S(1)}, bf16[1024,128]{1,0:T(8,128)(2,1)S(1)}, u32[]{:S(2)}, u32[]{:S(2)}) %collective-permute-start.16) | collective-permute-done | bytes 262176 | tf_op jit(solution)/shard_map/ppermute | solution.py:478
  51.2 0.8 %shard_map.95 = bf16[1024,128]{1,0:T(8,128)(2,1)} custom-call(bf16[1024,128]{1,0:T(8,128)(2,1)S(1)} %get-tuple-element.34.h_ref, f32[1024,128]{1,0:T(8,128)S(1)} %get-tuple-element.61.a_ref, bf16[1024,128]{1,0:T(8,128)(2,1)S(1)} %collective-permute-done.16.b_ref), custom_call_target="tpu_custom_call" | custom-call | tf_op jit(solution)/shard_map/pallas_call | solution.py:52
  (11 shorter events, 0.2 us)
Async XLA Ops:
  2.0 6.7 %collective-permute-start = (bf16[640,128]{1,0:T(8,128)(2,1)S(1)}, bf16[640,128]{1,0:T(8,128)(2,1)S(1)}, u32[]{:S(2)}, u32[]{:S(2)}) collective-permute-start(bf16[640,128]{1,0:T(8,128)(2,1)S(1)} %get-tuple-element.41), channel_id=1, source_target_pairs={{0,8},{1,3},{2,10},{3,1},{4,12},{5,7},{6,14},{7,5},{8,0},{9,11},{1... | collective-permute-start | bytes 491528 | tf_op jit(solution)/shard_map/ppermute | solution.py:475
  5.8 7.0 %copy-start.2 = (s32[3,4096]{1,0:T(4,128)S(1)}, s32[3,4096]{1,0:T(4,128)}, u32[]{:S(2)}) copy-start(s32[3,4096]{1,0:T(4,128)} %wave_ref.1) | copy-start | bytes 147460
  5.8 5.4 %collective-permute-start.7 = (bf16[640,128]{1,0:T(8,128)(2,1)S(1)}, bf16[640,128]{1,0:T(8,128)(2,1)S(1)}, u32[]{:S(2)}, u32[]{:S(2)}) collective-permute-start(bf16[640,128]{1,0:T(8,128)(2,1)S(1)} %get-tuple-element.51), channel_id=1, source_target_pairs={{0,2},{1,5},{2,0},{3,7},{4,6},{5,1},{6,4},{7,3},{8,10},{9,13},{10,... | collective-permute-start | bytes 491528 | tf_op jit(solution)/shard_map/ppermute | solution.py:475
  7.4 5.5 %copy-start = (f32[1,4096,128]{2,1,0:T(8,128)S(1)}, f32[1,4096,128]{2,1,0:T(8,128)}, u32[]{:S(2)}) copy-start(f32[1,4096,128]{2,1,0:T(8,128)} %param.13) | copy-start | bytes 6291460
  8.7 5.1 %collective-permute-start.1 = (bf16[320,128]{1,0:T(8,128)(2,1)S(1)}, bf16[320,128]{1,0:T(8,128)(2,1)S(1)}, u32[]{:S(2)}, u32[]{:S(2)}) collective-permute-start(bf16[320,128]{1,0:T(8,128)(2,1)S(1)} %get-tuple-element.43), channel_id=1, source_target_pairs={{0,4},{1,5},{2,6},{3,7},{4,0},{5,1},{6,2},{7,3},{8,12},{9,13},{10,... | collective-permute-start | bytes 245768 | tf_op jit(solution)/shard_map/ppermute | solution.py:475
  11.3 4.5 %collective-permute-start.8 = (bf16[320,128]{1,0:T(8,128)(2,1)S(1)}, bf16[320,128]{1,0:T(8,128)(2,1)S(1)}, u32[]{:S(2)}, u32[]{:S(2)}) collective-permute-start(bf16[320,128]{1,0:T(8,128)(2,1)S(1)} %get-tuple-element.53), channel_id=1, source_target_pairs={{0,4},{1,9},{2,6},{3,11},{4,0},{5,13},{6,2},{7,15},{8,12},{9,1},{1... | collective-permute-start | bytes 245768 | tf_op jit(solution)/shard_map/ppermute | solution.py:475
  12.9 11.3 %copy-start.1 = (f32[1,128,128]{2,1,0:T(8,128)S(1)}, f32[1,128,128]{2,1,0:T(8,128)}, u32[]{:S(2)}) copy-start(f32[1,128,128]{2,1,0:T(8,128)} %param.12) | copy-start | bytes 196612
  13.8 4.1 %collective-permute-start.2 = (bf16[160,128]{1,0:T(8,128)(2,1)S(1)}, bf16[160,128]{1,0:T(8,128)(2,1)S(1)}, u32[]{:S(2)}, u32[]{:S(2)}) collective-permute-start(bf16[160,128]{1,0:T(8,128)(2,1)S(1)} %get-tuple-element.45), channel_id=1, source_target_pairs={{0,2},{1,9},{2,0},{3,11},{4,6},{5,13},{6,4},{7,15},{8,10},{9,1},{1... | collective-permute-start | bytes 122888 | tf_op jit(solution)/shard_map/ppermute | solution.py:475
  15.3 7.2 %collective-permute-start.4 = (f32[160,128]{1,0:T(8,128)S(1)}, f32[160,128]{1,0:T(8,128)S(1)}, u32[]{:S(2)}, u32[]{:S(2)}) collective-permute-start(f32[160,128]{1,0:T(8,128)S(1)} %get-tuple-element.49), channel_id=1, source_target_pairs={{0,1},{1,0},{2,3},{3,2},{4,5},{5,4},{6,7},{7,6},{8,9},{9,8},{10,11... | collective-permute-start | bytes 245768 | tf_op jit(solution)/shard_map/ppermute | solution.py:478
  15.8 29.4 %copy-start.3 = (bf16[1,128,128]{2,1,0:T(8,128)(2,1)S(1)}, bf16[1,128,128]{2,1,0:T(8,128)(2,1)}, u32[]{:S(2)}) copy-start(bf16[1,128,128]{2,1,0:T(8,128)(2,1)} %param.11) | copy-start | bytes 98308
  15.8 29.4 %copy-start.4 = (s32[8,8]{1,0:T(8,128)S(1)}, s32[8,8]{1,0:T(8,128)}, u32[]{:S(2)}) copy-start(s32[8,8]{1,0:T(8,128)} %refs_1_.1) | copy-start | bytes 772
  15.8 4.7 %collective-permute-start.9 = (bf16[160,128]{1,0:T(8,128)(2,1)S(1)}, bf16[160,128]{1,0:T(8,128)(2,1)S(1)}, u32[]{:S(2)}, u32[]{:S(2)}) collective-permute-start(bf16[160,128]{1,0:T(8,128)(2,1)S(1)} %get-tuple-element.55), channel_id=1, source_target_pairs={{0,8},{1,3},{2,10},{3,1},{4,12},{5,7},{6,14},{7,5},{8,0},{9,11},{1... | collective-permute-start | bytes 122888 | tf_op jit(solution)/shard_map/ppermute | solution.py:475
  17.9 6.3 %collective-permute-start.3 = (bf16[160,128]{1,0:T(8,128)(2,1)S(1)}, bf16[160,128]{1,0:T(8,128)(2,1)S(1)}, u32[]{:S(2)}, u32[]{:S(2)}) collective-permute-start(bf16[160,128]{1,0:T(8,128)(2,1)S(1)} %get-tuple-element.47), channel_id=1, source_target_pairs={{0,16},{1,17},{2,18},{3,19},{4,20},{5,21},{6,22},{7,23},{8,24},{9,... | collective-permute-start | bytes 122888 | tf_op jit(solution)/shard_map/ppermute | solution.py:475
  20.5 5.3 %collective-permute-start.10 = (bf16[160,128]{1,0:T(8,128)(2,1)S(1)}, bf16[160,128]{1,0:T(8,128)(2,1)S(1)}, u32[]{:S(2)}, u32[]{:S(2)}) collective-permute-start(bf16[160,128]{1,0:T(8,128)(2,1)S(1)} %get-tuple-element.57), channel_id=1, source_target_pairs={{0,16},{1,17},{2,18},{3,19},{4,20},{5,21},{6,22},{7,23},{8,24},{9,... | collective-permute-start | bytes 122888 | tf_op jit(solution)/shard_map/ppermute | solution.py:475
  24.4 4.1 %collective-permute-start.5 = (bf16[160,128]{1,0:T(8,128)(2,1)S(1)}, bf16[160,128]{1,0:T(8,128)(2,1)S(1)}, u32[]{:S(2)}, u32[]{:S(2)}) collective-permute-start(bf16[160,128]{1,0:T(8,128)(2,1)S(1)} %shard_map.80.a_ref), channel_id=1, source_target_pairs={{0,2},{1,9},{2,0},{3,11},{4,6},{5,13},{6,4},{7,15},{8,10},{9,1},{1... | collective-permute-start | bytes 122888 | tf_op jit(solution)/shard_map/ppermute | solution.py:475
  26.1 4.3 %collective-permute-start.11 = (bf16[160,128]{1,0:T(8,128)(2,1)S(1)}, bf16[160,128]{1,0:T(8,128)(2,1)S(1)}, u32[]{:S(2)}, u32[]{:S(2)}) collective-permute-start(bf16[160,128]{1,0:T(8,128)(2,1)S(1)} %shard_map.87.a_ref), channel_id=1, source_target_pairs={{0,8},{1,3},{2,10},{3,1},{4,12},{5,7},{6,14},{7,5},{8,0},{9,11},{1... | collective-permute-start | bytes 122888 | tf_op jit(solution)/shard_map/ppermute | solution.py:475
  28.4 4.4 %collective-permute-start.6 = (bf16[320,128]{1,0:T(8,128)(2,1)S(1)}, bf16[320,128]{1,0:T(8,128)(2,1)S(1)}, u32[]{:S(2)}, u32[]{:S(2)}) collective-permute-start(bf16[320,128]{1,0:T(8,128)(2,1)S(1)} %shard_map.81.a_ref), channel_id=1, source_target_pairs={{0,4},{1,5},{2,6},{3,7},{4,0},{5,1},{6,2},{7,3},{8,12},{9,13},{10,... | collective-permute-start | bytes 245768 | tf_op jit(solution)/shard_map/ppermute | solution.py:475
  30.3 5.3 %collective-permute-start.12 = (bf16[320,128]{1,0:T(8,128)(2,1)S(1)}, bf16[320,128]{1,0:T(8,128)(2,1)S(1)}, u32[]{:S(2)}, u32[]{:S(2)}) collective-permute-start(bf16[320,128]{1,0:T(8,128)(2,1)S(1)} %shard_map.88.a_ref), channel_id=1, source_target_pairs={{0,4},{1,9},{2,6},{3,11},{4,0},{5,13},{6,2},{7,15},{8,12},{9,1},{1... | collective-permute-start | bytes 245768 | tf_op jit(solution)/shard_map/ppermute | solution.py:475
  32.9 15.5 %collective-permute-start.13 = (bf16[640,128]{1,0:T(8,128)(2,1)S(1)}, bf16[640,128]{1,0:T(8,128)(2,1)S(1)}, u32[]{:S(2)}, u32[]{:S(2)}) collective-permute-start(bf16[640,128]{1,0:T(8,128)(2,1)S(1)} %shard_map.82.refs_0_), channel_id=1, source_target_pairs={{0,8},{1,3},{2,10},{3,1},{4,12},{5,7},{6,14},{7,5},{8,0},{9,11},{1... | collective-permute-start | bytes 491528 | tf_op jit(solution)/shard_map/ppermute | solution.py:475
  35.7 13.2 %collective-permute-start.14 = (bf16[640,128]{1,0:T(8,128)(2,1)S(1)}, bf16[640,128]{1,0:T(8,128)(2,1)S(1)}, u32[]{:S(2)}, u32[]{:S(2)}) collective-permute-start(bf16[640,128]{1,0:T(8,128)(2,1)S(1)} %shard_map.89.refs_1_), channel_id=1, source_target_pairs={{0,2},{1,5},{2,0},{3,7},{4,6},{5,1},{6,4},{7,3},{8,10},{9,13},{10,... | collective-permute-start | bytes 491528 | tf_op jit(solution)/shard_map/ppermute | solution.py:475
  37.0 8.2 %collective-permute-start.15 = (bf16[560,128]{1,0:T(8,128)(2,1)S(1)}, bf16[560,128]{1,0:T(8,128)(2,1)S(1)}, u32[]{:S(2)}, u32[]{:S(2)}) collective-permute-start(bf16[560,128]{1,0:T(8,128)(2,1)S(1)} %shard_map.92), channel_id=1, source_target_pairs={{0,31},{1,2},{2,1},{3,4},{4,3},{5,6},{6,5},{7,8},{8,7},{9,10},{10,... | collective-permute-start | bytes 430088 | tf_op jit(solution)/shard_map/ppermute | solution.py:493
  49.6 1.6 %collective-permute-start.16 = (bf16[1024,128]{1,0:T(8,128)(2,1)S(1)}, bf16[1024,128]{1,0:T(8,128)(2,1)S(1)}, u32[]{:S(2)}, u32[]{:S(2)}) collective-permute-start(bf16[1024,128]{1,0:T(8,128)(2,1)S(1)} %get-tuple-element.62), channel_id=1, source_target_pairs={{0,1},{1,0},{2,3},{3,2},{4,5},{5,4},{6,7},{7,6},{8,9},{9,8},{10,11... | collective-permute-start | bytes 786440 | tf_op jit(solution)/shard_map/ppermute | solution.py:478
